TPU v7x, 32 devices: a whole 2x2x4 slice. The times are simulated.
32 devices in a mesh: grp: 4 (over y, core), dom: 8 (over z, x).
Axes of the slice: x: 2, y: 2, z: 4, core: 2. Of those that a mesh axis runs over, the one named last changes fastest.
Arguments:
- entity: bfloat16 [65536, 256], P(('grp', 'dom')), may hold values from -1.5 to 1.5
- entity_acc: float32 [65536], P(('grp', 'dom')), may hold values from 0.1 to 1
- relation: float32 [1000, 256], replicated, may hold values from -3 to 3
- rel_acc: float32 [1000], replicated, may hold values from 0.1 to 1
- edge_src: int32 [32, 2, 3072], P(('grp', 'dom')), may hold values from 0 to 2047
- edge_rel: int32 [32, 2, 3072], P(('grp', 'dom')), may hold values from 0 to 999
- edge_dst: int32 [32, 2, 3072], P(('grp', 'dom')), may hold values from 0 to 2047
- negatives: int32 [32, 2, 6, 512], P(('grp', 'dom')), may hold values from 0 to 2047
Outputs:
- entity_new: bfloat16 [65536, 256], P(('grp', 'dom'))
- entity_acc_new: float32 [65536], P(('grp', 'dom'))
- relation_new: float32 [1000, 256], replicated
- rel_acc_new: float32 [1000], replicated
All inputs are finite; a program needn't handle non-finite values.
Results may differ from a plain program's by a relative error of at most 0.0042.
Values may be sent and summed in bfloat16 or wider, within the bound.
No kernel may reach another device: no remote copies, remote signals or barrier semaphores. Data moves between devices by JAX's collectives and lax.ppermute only.
A program may use at most 128 MiB of HBM per device.

v0:
```python
import jax
import jax.numpy as jnp
from jax import lax
from jax.experimental import pallas as pl
from jax.experimental.pallas import tpu as pltpu
from jax.sharding import PartitionSpec as P

learn_rate = 0.3
bf16 = jnp.bfloat16
f32 = jnp.float32


def passed_along(block, axis, distance):
    devices = range(lax.axis_size(axis))
    route = [((i - distance) % len(devices), i) for i in devices]
    return lax.ppermute(block, axis, route)


def dot_nn(a, b):
    return jnp.dot(a, b, preferred_element_type=f32)


def dot_nt(a, b):
    return lax.dot_general(a, b, (((1,), (1,)), ((), ())), preferred_element_type=f32)


def one_hot(ids, rows):
    shape = (rows, ids.shape[1])
    match = ids.astype(jnp.int16) == lax.broadcasted_iota(jnp.int16, shape, 0)
    return jnp.where(match, jnp.ones((), bf16), jnp.zeros((), bf16))


def bucket_kernel(ids_ref, left_ref, right_ref, rel_ref, rel_in_ref, d_left_ref, d_right_ref, d_rel_ref, right_sum):
    step = pl.program_id(0)
    features, rows = left_ref.shape
    middle = features // 2
    n_rel = rel_ref.shape[1]

    @pl.when(step == 0)
    def _():
        d_left_ref[...] = jnp.zeros_like(d_left_ref)
        d_rel_ref[...] = rel_in_ref[...]
        right_sum[...] = jnp.zeros_like(right_sum)

    ids = ids_ref[0]
    pick_source = one_hot(ids[0:1], rows)
    heads = dot_nn(left_ref[...], pick_source)
    pick_rel = one_hot(ids[1:2], n_rel)
    both = dot_nn(rel_ref[...], pick_rel)
    rel = both[:features] + both[features:]
    h_re, h_im = heads[:middle], heads[middle:]
    r_re, r_im = rel[:middle], rel[middle:]
    query = jnp.concatenate([h_re * r_re - h_im * r_im, h_re * r_im + h_im * r_re], 0).astype(bf16)

    pick_target = one_hot(ids[2:3], rows)
    tails = dot_nn(right_ref[...], pick_target)
    pick_neg = one_hot(ids[3:4], rows)
    cands = dot_nn(right_ref[...], pick_neg).astype(bf16)

    query32 = query.astype(f32)
    positive = jnp.sum(query32 * tails, axis=0, keepdims=True)
    scores = dot_nn(cands.T, query)
    peak = jnp.maximum(jnp.max(scores, axis=0, keepdims=True), positive)
    expd = jnp.exp(scores - peak)
    own = jnp.exp(positive - peak)
    inverse = 1.0 / (own + jnp.sum(expd, axis=0, keepdims=True))
    shares = (expd * inverse).astype(bf16)
    coefficient = own * inverse - 1.0

    d_cands = dot_nt(query, shares).astype(bf16)
    d_tails = (coefficient * query32).astype(bf16)
    right_sum[...] += dot_nt(pick_target, d_tails) + dot_nt(pick_neg, d_cands)

    grad = coefficient * tails + dot_nn(cands, shares)
    g_re, g_im = grad[:middle], grad[middle:]
    d_heads = jnp.concatenate([g_re * r_re + g_im * r_im, g_im * r_re - g_re * r_im], 0).astype(bf16)
    d_left_ref[...] += dot_nt(pick_source, d_heads)
    d_rels = jnp.concatenate([g_re * h_re + g_im * h_im, g_im * h_re - g_re * h_im], 0).astype(bf16)
    d_rel_ref[...] += dot_nt(pick_rel, d_rels)

    @pl.when(step == pl.num_programs(0) - 1)
    def _():
        d_right_ref[...] = right_sum[...].astype(bf16)


def bucket(ids, left, right, rel, rel_sum):
    spans, _, span = ids.shape
    features, rows = left.shape
    n_rel = rel.shape[1]

    def whole(shape):
        return pl.BlockSpec(shape, lambda s: (0,) * len(shape))

    return pl.pallas_call(
        bucket_kernel,
        grid=(spans,),
        in_specs=[
            pl.BlockSpec((1, 4, span), lambda s: (s, 0, 0)),
            whole((features, rows)),
            whole((features, rows)),
            whole((2 * features, n_rel)),
            whole((n_rel, features)),
        ],
        out_specs=[whole((rows, features)), whole((rows, features)), whole((n_rel, features))],
        out_shape=[
            jax.ShapeDtypeStruct((rows, features), f32),
            jax.ShapeDtypeStruct((rows, features), bf16),
            jax.ShapeDtypeStruct((n_rel, features), f32),
        ],
        scratch_shapes=[pltpu.VMEM((rows, features), f32)],
        compiler_params=pltpu.CompilerParams(
            dimension_semantics=("arbitrary",), vmem_limit_bytes=52 << 20
        ),
        cost_estimate=pl.CostEstimate(
            flops=2 * spans * span * features * (6 * rows + 3 * n_rel + 3 * span),
            bytes_accessed=14 << 20,
            transcendentals=spans * span * span,
        ),
        name="bucket",
    )(ids, left, right, rel, rel_sum)


def relation_total(partial, axes):
    devices = 1
    for axis in axes:
        devices *= lax.axis_size(axis)
    rows, features = partial.shape
    blocks = partial.astype(bf16).reshape(devices, rows // devices, features)
    mine = lax.all_to_all(blocks, axes, 0, 0, tiled=True)
    mine = jnp.sum(mine.astype(f32), axis=0).astype(bf16)
    spread = jnp.broadcast_to(mine[None], blocks.shape)
    return lax.all_to_all(spread, axes, 0, 0, tiled=True).reshape(rows, features).astype(f32)


def body(entity, entity_acc, relation, rel_acc, edge_src, edge_rel, edge_dst, negatives):
    axes = ("grp", "dom")
    half_group = lax.axis_size("dom") // 2
    n_rel, features = relation.shape
    spans, span = negatives.shape[2:]
    devices = lax.axis_size("grp") * lax.axis_size("dom")
    rel_rows = -(-n_rel // max(128, 8 * devices)) * max(128, 8 * devices)

    own = entity.T
    inner_block = passed_along(own, "dom", half_group)
    outer_block = passed_along(own, "grp", 1)
    padded = jnp.pad(relation, ((0, rel_rows - n_rel), (0, 0))).T
    rel_high = padded.astype(bf16)
    rel_low = (padded - rel_high.astype(f32)).astype(bf16)
    rel = jnp.concatenate([rel_high, rel_low], axis=0)
    ids = jnp.stack(
        [a[0].reshape(2, spans, span) for a in (edge_src, edge_rel, edge_dst, negatives)], axis=2
    )

    left_two, right_two, rel_sum = bucket(
        ids[1], own, outer_block, rel, jnp.zeros((rel_rows, features), f32)
    )
    back_outer = passed_along(right_two, "grp", -1)
    left_one, right_one, rel_sum = bucket(ids[0], own, inner_block, rel, rel_sum)
    back_inner = passed_along(right_one, "dom", half_group)
    row_grad = left_one + left_two + back_inner.astype(f32) + back_outer.astype(f32)
    entity_acc_new = entity_acc + jnp.mean(row_grad * row_grad, axis=1)
    entity_new = (
        entity.astype(f32) - learn_rate * row_grad / jnp.sqrt(entity_acc_new)[:, None]
    ).astype(bf16)
    rel_total = relation_total(rel_sum, axes)[:n_rel]
    rel_acc_new = rel_acc + jnp.mean(rel_total * rel_total, axis=1)
    relation_new = relation - learn_rate * rel_total / jnp.sqrt(rel_acc_new)[:, None]
    return (entity_new, entity_acc_new, relation_new, rel_acc_new)


def solution(mesh):
    return jax.shard_map(
        body,
        mesh=mesh,
        in_specs=(
            P(("grp", "dom"), None),
            P(("grp", "dom")),
            P(),
            P(),
            P(("grp", "dom"), None, None),
            P(("grp", "dom"), None, None),
            P(("grp", "dom"), None, None),
            P(("grp", "dom"), None, None, None),
        ),
        out_specs=(P(("grp", "dom"), None), P(("grp", "dom")), P(), P()),
        check_vma=False,
    )
```

profile of v0, /device:TPU:0, one launch (start us, length us, event | category | flops | bytes accessed | tf_op | source)
XLA Modules:
  0.0 178.7 jit_solution(11859701984397619286)
XLA Ops:
  0.6 0.0 copy-start.6
  0.6 0.0 copy-start.7
  0.7 0.0 copy-start.8
  0.7 0.0 copy-start.9
  0.7 0.0 copy-start.3
  0.7 1.6 copy.13
  2.3 0.0 copy-start.5
  2.3 0.5 collective-permute-start.1
  2.8 3.7 %collective-permute-start = (bf16[256,2048]{1,0:T(8,128)(2,1)S(1)}, bf16[256,2048]{1,0:T(8,128)(2,1)}, u32[]{:S(2)}, u32[]{:S(2)}) collective-permute-start(bf16[256,2048]{1,0:T(8,128)(2,1)S(1)} %bitcast.21), channel_id=1, source_target_pairs={{4,0},{5,1},{6,2},{7,3},{0,4},{1,5},{2,6},{3,7},{12,8},{13,9},{14,... | collective-permute-start | bytes 3145736 | tf_op jit(solution)/shard_map/ppermute | solution.py:16
  6.4 0.0 copy-done.6
  6.5 0.0 copy-done.7
  6.6 0.0 copy-done.8
  6.6 0.0 copy-done.9
  6.7 0.0 copy-done.3
  6.7 0.3 copy.14
  7.0 0.1 pad_add_fusion
  7.1 0.1 fusion
  7.2 0.1 bitcast_convert_fusion
  7.3 0.0 copy-done.5
  7.3 1.0 pad_maximum_fusion.rel_ref
  8.3 9.0 %collective-permute-done.1.right_ref = bf16[256,2048]{1,0:T(8,128)(2,1)} collective-permute-done((bf16[256,2048]{1,0:T(8,128)(2,1)S(1)}, bf16[256,2048]{1,0:T(8,128)(2,1)}, u32[]{:S(2)}, u32[]{:S(2)}) %collective-permute-start.1) | collective-permute-done | bytes 1048608 | tf_op jit(solution)/shard_map/ppermute | solution.py:16
  17.3 1.1 broadcast_in_dim.4.rel_in_ref
  18.4 38.1 %bucket.2 = (f32[2048,256]{1,0:T(8,128)}, bf16[2048,256]{1,0:T(8,128)(2,1)S(1)}, f32[1024,256]{1,0:T(8,128)}) custom-call(s32[6,4,512]{2,1,0:T(4,128)S(1)} %get-tuple-element.21.ids_ref, bf16[256,2048]{1,0:T(8,128)(2,1)} %bitcast.22, bf16[256,2048]{1,0:T(8,128)(2,1)} %collective-permute-done.1.right_ref, bf16[512,1024]{1,0:T(8,128)(2,1)} %pad_maximum_fusion.rel_ref, ...), custom_call_target="tpu_custom_call" | custom-call | flops 26575110144 | bytes 14680064 | tf_op jit(solution)/shard_map/bucket/pallas_call | solution.py:94
  56.4 0.0 collective-permute-done.right_ref
  56.4 38.1 %bucket.3 = (f32[2048,256]{1,0:T(8,128)}, bf16[2048,256]{1,0:T(8,128)(2,1)S(1)}, f32[1024,256]{1,0:T(8,128)}) custom-call(s32[6,4,512]{2,1,0:T(4,128)S(1)} %get-tuple-element.20.ids_ref, bf16[256,2048]{1,0:T(8,128)(2,1)} %bitcast.23, bf16[256,2048]{1,0:T(8,128)(2,1)} %collective-permute-done.right_ref, bf16[512,1024]{1,0:T(8,128)(2,1)} %pad_maximum_fusion.rel_ref, ...), custom_call_target="tpu_custom_call" | custom-call | flops 26575110144 | bytes 14680064 | tf_op jit(solution)/shard_map/bucket/pallas_call | solution.py:94
  94.5 3.4 %collective-permute-start.2 = (bf16[2048,256]{1,0:T(8,128)(2,1)S(1)}, bf16[2048,256]{1,0:T(8,128)(2,1)}, u32[]{:S(2)}, u32[]{:S(2)}) collective-permute-start(bf16[2048,256]{1,0:T(8,128)(2,1)S(1)} %get-tuple-element.13), channel_id=1, source_target_pairs={{4,0},{5,1},{6,2},{7,3},{0,4},{1,5},{2,6},{3,7},{12,8},{13,9},{14,... | collective-permute-start | bytes 3145736 | tf_op jit(solution)/shard_map/ppermute | solution.py:16
  97.9 0.0 collective-permute-start.3
  97.9 1.3 convert_element_type.39
  99.2 54.5 %all_to_all.10 = bf16[32,32,256]{2,1,0:T(8,128)(2,1)S(1)} all-to-all(bf16[32,32,256]{2,1,0:T(8,128)(2,1)S(1)} %bitcast.19), channel_id=1, replica_groups=mesh['grp'=4,'dom'=8] {'grp','dom'}, dimensions={0} | all-to-all | bytes 1048576 | tf_op jit(solution)/shard_map/all_to_all | solution.py:129
  153.7 0.1 reduce_sum.31
  153.8 0.9 broadcast_in_dim.5
  154.6 5.7 %all-to-all-start.1 = ((bf16[32,32,256]{2,1,0:T(8,128)(2,1)}), bf16[32,32,256]{2,1,0:T(8,128)(2,1)S(1)}, u32[]{:S(2)}, u32[]{:S(2)}) async-start(bf16[32,32,256]{2,1,0:T(8,128)(2,1)} %broadcast_in_dim.5), calls=%async_computation.1 | async-start | bytes 1048576 | tf_op jit(solution)/shard_map/all_to_all | solution.py:132
  160.4 0.0 collective-permute-done.2
  160.4 0.0 collective-permute-done.3
  160.4 0.0 copy-start.10
  160.4 0.0 copy-start
  160.4 0.0 copy-start.1
  160.4 0.0 copy-start.2
  160.4 3.6 %multiply_reduce_fusion = f32[2048]{0:T(1024)S(1)} fusion(bf16[2048,256]{1,0:T(8,128)(2,1)} %collective-permute-done.3, bf16[2048,256]{1,0:T(8,128)(2,1)} %collective-permute-done.2, f32[2048,256]{1,0:T(8,128)} %get-tuple-element.11, f32[2048,256]{1,0:T(8,128)} %get-tuple-element.12), kind=kLoop, calls=%fused_computation.1 | loop fusion | flops 3667968 | bytes 6299648 | tf_op jit(solution)/shard_map/reduce_sum | solution.py:161
  164.0 0.0 copy-done.10
  164.0 0.6 fusion.5
  164.6 0.0 copy-done
  164.6 0.0 copy-done.1
  164.6 0.1 copy-done.2
  164.7 0.0 copy-start.11
  164.7 0.0 copy-start.4
  164.8 3.4 %subtract_convert_fusion = bf16[2048,256]{1,0:T(8,128)(2,1)} fusion(bf16[2048,256]{1,0:T(8,128)(2,1)S(1)} %copy-done.2, f32[2048]{0:T(1024)S(1)} %get-tuple-element.18, bf16[2048,256]{1,0:T(8,128)(2,1)} %collective-permute-done.3, bf16[2048,256]{1,0:T(8,128)(2,1)} %collective-permute-done.2, f32[2048,256]{1,0:T(8,128)S(1)} %copy-done.1, f32[2048,256]{1,0:T(8,128)S(1)} %copy-done), kind=kLoop, calls=%fused_computation | loop fusion | flops 5242880 | bytes 8396800 | tf_op jit(solution)/shard_map/convert_element_type | solution.py:164
  168.1 8.6 %all-to-all-done.1 = bf16[32,32,256]{2,1,0:T(8,128)(2,1)S(1)} async-done(((bf16[32,32,256]{2,1,0:T(8,128)(2,1)}), bf16[32,32,256]{2,1,0:T(8,128)(2,1)S(1)}, u32[]{:S(2)}, u32[]{:S(2)}) %all-to-all-start.1) | async-done | bytes 524320 | tf_op jit(solution)/shard_map/all_to_all | solution.py:132
  176.7 0.2 fusion.3
  176.9 0.0 copy-done.11
  176.9 0.6 fusion.4
  177.5 0.0 copy-done.4
  177.5 1.2 fusion.2
  (5 shorter events, 0.2 us)
Async XLA Ops:
  0.6 5.8 %copy-start.6 = (s32[1,2,3072]{2,1,0:T(2,128)S(1)}, s32[1,2,3072]{2,1,0:T(2,128)}, u32[]{:S(2)}) copy-start(s32[1,2,3072]{2,1,0:T(2,128)} %param.12) | copy-start | bytes 73732
  0.6 5.9 %copy-start.7 = (s32[1,2,3072]{2,1,0:T(2,128)S(1)}, s32[1,2,3072]{2,1,0:T(2,128)}, u32[]{:S(2)}) copy-start(s32[1,2,3072]{2,1,0:T(2,128)} %param.13) | copy-start | bytes 73732
  0.7 5.9 %copy-start.8 = (s32[1,2,3072]{2,1,0:T(2,128)S(1)}, s32[1,2,3072]{2,1,0:T(2,128)}, u32[]{:S(2)}) copy-start(s32[1,2,3072]{2,1,0:T(2,128)} %param.14) | copy-start | bytes 73732
  0.7 6.0 %copy-start.9 = (s32[1,2,6,512]{3,1,2,0:T(2,128)S(1)}, s32[1,2,6,512]{3,1,2,0:T(2,128)}, u32[]{:S(2)}) copy-start(s32[1,2,6,512]{3,1,2,0:T(2,128)} %param.15) | copy-start | bytes 73732
  0.7 6.0 %copy-start.3 = (f32[1000,256]{1,0:T(8,128)S(1)}, f32[1000,256]{1,0:T(8,128)}, u32[]{:S(2)}) copy-start(f32[1000,256]{1,0:T(8,128)} %param.10) | copy-start | bytes 3072004
  2.3 5.0 %copy-start.5 = (bf16[2048,256]{0,1:T(8,128)(2,1)}, bf16[2048,256]{0,1:T(8,128)(2,1)S(1)}, u32[]{:S(2)}) copy-start(bf16[2048,256]{0,1:T(8,128)(2,1)S(1)} %copy.13) | copy-start | bytes 3145732
  2.3 15.0 %collective-permute-start.1 = (bf16[256,2048]{1,0:T(8,128)(2,1)S(1)}, bf16[256,2048]{1,0:T(8,128)(2,1)}, u32[]{:S(2)}, u32[]{:S(2)}) collective-permute-start(bf16[256,2048]{1,0:T(8,128)(2,1)S(1)} %bitcast.20), channel_id=1, source_target_pairs={{24,0},{0,8},{8,16},{16,24},{25,1},{1,9},{9,17},{17,25},{26,2},{2,... | collective-permute-start | bytes 3145736 | tf_op jit(solution)/shard_map/ppermute | solution.py:16
  2.8 53.7 %collective-permute-start = (bf16[256,2048]{1,0:T(8,128)(2,1)S(1)}, bf16[256,2048]{1,0:T(8,128)(2,1)}, u32[]{:S(2)}, u32[]{:S(2)}) collective-permute-start(bf16[256,2048]{1,0:T(8,128)(2,1)S(1)} %bitcast.21), channel_id=1, source_target_pairs={{4,0},{5,1},{6,2},{7,3},{0,4},{1,5},{2,6},{3,7},{12,8},{13,9},{14,... | collective-permute-start | bytes 3145736 | tf_op jit(solution)/shard_map/ppermute | solution.py:16
  94.5 65.8 %collective-permute-start.2 = (bf16[2048,256]{1,0:T(8,128)(2,1)S(1)}, bf16[2048,256]{1,0:T(8,128)(2,1)}, u32[]{:S(2)}, u32[]{:S(2)}) collective-permute-start(bf16[2048,256]{1,0:T(8,128)(2,1)S(1)} %get-tuple-element.13), channel_id=1, source_target_pairs={{4,0},{5,1},{6,2},{7,3},{0,4},{1,5},{2,6},{3,7},{12,8},{13,9},{14,... | collective-permute-start | bytes 3145736 | tf_op jit(solution)/shard_map/ppermute | solution.py:16
  97.9 62.5 %collective-permute-start.3 = (bf16[2048,256]{1,0:T(8,128)(2,1)S(1)}, bf16[2048,256]{1,0:T(8,128)(2,1)}, u32[]{:S(2)}, u32[]{:S(2)}) collective-permute-start(bf16[2048,256]{1,0:T(8,128)(2,1)S(1)} %get-tuple-element.14), channel_id=1, source_target_pairs={{8,0},{16,8},{24,16},{0,24},{9,1},{17,9},{25,17},{1,25},{10,2},{18... | collective-permute-start | bytes 3145736 | tf_op jit(solution)/shard_map/ppermute | solution.py:16
  154.6 22.1 %all-to-all-start.1 = ((bf16[32,32,256]{2,1,0:T(8,128)(2,1)}), bf16[32,32,256]{2,1,0:T(8,128)(2,1)S(1)}, u32[]{:S(2)}, u32[]{:S(2)}) async-start(bf16[32,32,256]{2,1,0:T(8,128)(2,1)} %broadcast_in_dim.5), calls=%async_computation.1 | async-start | bytes 1048576 | tf_op jit(solution)/shard_map/all_to_all | solution.py:132
  160.4 3.6 %copy-start.10 = (f32[2048]{0:T(1024)S(1)}, f32[2048]{0:T(1024)}, u32[]{:S(2)}) copy-start(f32[2048]{0:T(1024)} %param.9) | copy-start | bytes 24580
  160.4 4.2 %copy-start = (f32[2048,256]{1,0:T(8,128)S(1)}, f32[2048,256]{1,0:T(8,128)}, u32[]{:S(2)}) copy-start(f32[2048,256]{1,0:T(8,128)} %get-tuple-element.12) | copy-start | bytes 6291460
  160.4 4.2 %copy-start.1 = (f32[2048,256]{1,0:T(8,128)S(1)}, f32[2048,256]{1,0:T(8,128)}, u32[]{:S(2)}) copy-start(f32[2048,256]{1,0:T(8,128)} %get-tuple-element.11) | copy-start | bytes 6291460
  160.4 4.3 %copy-start.2 = (bf16[2048,256]{1,0:T(8,128)(2,1)S(1)}, bf16[2048,256]{1,0:T(8,128)(2,1)}, u32[]{:S(2)}) copy-start(bf16[2048,256]{1,0:T(8,128)(2,1)} %param.8) | copy-start | bytes 3145732
  164.7 12.2 %copy-start.11 = (f32[1000]{0:T(1024)S(1)}, f32[1000]{0:T(1024)}, u32[]{:S(2)}) copy-start(f32[1000]{0:T(1024)} %param.11) | copy-start | bytes 12004
  164.7 12.8 %copy-start.4 = (f32[1000,256]{1,0:T(8,128)S(1)}, f32[1000,256]{1,0:T(8,128)}, u32[]{:S(2)}) copy-start(f32[1000,256]{1,0:T(8,128)} %param.10) | copy-start | bytes 3072004
where the time goes:
time: 179 us
  Pallas kernels  76.1 us (43%)
  blocking collectives  54.5 us (30%)
  waiting for transfers between devices  17.6 us (10%)
  starting transfers between devices  13.2 us (7%)
  other arithmetic  12.1 us (7%)
  local copies, waits for them, and re-layouts  4.24 us (2%)
    pallas_call x2, Pallas kernels, bucket(): pl.pallas_call(bucket_kernel, grid=(spans,), in_specs=[pl.BlockSpec((1, 4...  76.1 us
    all_to_all x1, blocking collectives, relation_total(): mine = lax.all_to_all(blocks, axes, 0, 0, tiled=True)  54.5 us
    ppermute x4, waiting for transfers between devices, passed_along(): return lax.ppermute(block, axis, route)  9.01 us
    all_to_all x1, waiting for transfers between devices, relation_total(): lax.all_to_all(spread, axes, 0, 0, tiled=True).reshape(rows, features)  8.59 us
    ppermute x4, starting transfers between devices, passed_along(): return lax.ppermute(block, axis, route)  7.54 us
    all_to_all x1, starting transfers between devices, relation_total(): lax.all_to_all(spread, axes, 0, 0, tiled=True).reshape(rows, features)  5.7 us
  transfers between devices with their start and end apart: 5, of which 2 were waited for; matrix products, arithmetic and copies ran while one was open for 7% of the time, Pallas kernels for 21%

commit v1 on v0

v1 whole, which is shorter than its diff:
```python
import jax
import jax.numpy as jnp
from jax import lax
from jax.experimental import pallas as pl
from jax.experimental.pallas import tpu as pltpu
from jax.sharding import PartitionSpec as P

learn_rate = 0.3
bf16 = jnp.bfloat16
f32 = jnp.float32
VMEM_LIMIT = 52 << 20


def dot_nn(a, b):
    return jnp.dot(a, b, preferred_element_type=f32)


def dot_nt(a, b):
    return lax.dot_general(a, b, (((1,), (1,)), ((), ())), preferred_element_type=f32)


def one_hot(ids, rows, first=0):
    shape = (rows, ids.shape[1])
    match = (ids - first).astype(jnp.int16) == lax.broadcasted_iota(jnp.int16, shape, 0)
    return jnp.where(match, jnp.ones((), bf16), jnp.zeros((), bf16))


def whole(shape):
    return pl.BlockSpec(shape, lambda s: (0,) * len(shape))


def across(height, width):
    return pl.BlockSpec((height, width), lambda s: (0, s))


def params():
    return pltpu.CompilerParams(dimension_semantics=("arbitrary",), vmem_limit_bytes=VMEM_LIMIT)


def halves(a):
    middle = a.shape[0] // 2
    return a[:middle], a[middle:]


def make_query(source, rel_ids, left, rel_table):
    features, rows = left.shape
    heads = dot_nn(left, one_hot(source, rows))
    both = dot_nn(rel_table, one_hot(rel_ids, rel_table.shape[1]))
    rel = both[:features] + both[features:]
    h_re, h_im = halves(heads)
    r_re, r_im = halves(rel)
    query = jnp.concatenate([h_re * r_re - h_im * r_im, h_re * r_im + h_im * r_re], 0)
    return heads, rel, query.astype(bf16)


def make_gradients(targets, negatives, heads, rel, query, right, heads_out, tails_out, cands_out, rels_out):
    rows = right.shape[1]
    tails = dot_nn(right, one_hot(targets, rows))
    cands = dot_nn(right, one_hot(negatives, rows)).astype(bf16)
    query32 = query.astype(f32)
    positive = jnp.sum(query32 * tails, axis=0, keepdims=True)
    scores = dot_nn(cands.T, query)
    peak = jnp.maximum(jnp.max(scores, axis=0, keepdims=True), positive)
    expd = jnp.exp(scores - peak)
    own = jnp.exp(positive - peak)
    inverse = 1.0 / (own + jnp.sum(expd, axis=0, keepdims=True))
    shares = (expd * inverse).astype(bf16)
    coefficient = own * inverse - 1.0
    tails_out[...] = (coefficient * query32).astype(bf16)
    cands_out[...] = dot_nt(query, shares).astype(bf16)
    grad = coefficient * tails + dot_nn(cands, shares)
    g_re, g_im = halves(grad)
    r_re, r_im = halves(rel)
    h_re, h_im = halves(heads)
    heads_out[...] = jnp.concatenate(
        [g_re * r_re + g_im * r_im, g_im * r_re - g_re * r_im], 0
    ).astype(bf16)
    rels_out[...] = jnp.concatenate(
        [g_re * h_re + g_im * h_im, g_im * h_re - g_re * h_im], 0
    ).astype(bf16)


def query_kernel(ids_ref, left_ref, table_ref, heads_ref, rel_ref, query_ref):
    ids = ids_ref[...]
    heads, rel, query = make_query(ids[0:1], ids[1:2], left_ref[...], table_ref[...])
    heads_ref[...] = heads.astype(bf16)
    rel_ref[...] = rel
    query_ref[...] = query


def gradient_kernel(ids_ref, heads_ref, rel_ref, query_ref, right_ref, *outs):
    ids = ids_ref[...]
    heads = heads_ref[...].astype(f32)
    make_gradients(ids[2:3], ids[3:4], heads, rel_ref[...], query_ref[...], right_ref[...], *outs)


def paired_kernel(home_ref, ids_ref, own_ref, met_ref, passed_ref, table_ref, *rest):
    *outs, left = rest

    @pl.when(pl.program_id(0) == 0)
    def _():
        @pl.when(home_ref[0] == 1)
        def _():
            left[...] = own_ref[...]

        @pl.when(home_ref[0] == 0)
        def _():
            left[...] = passed_ref[...]

    ids = ids_ref[...]
    heads, rel, query = make_query(ids[0:1], ids[1:2], left[...], table_ref[...])
    make_gradients(ids[2:3], ids[3:4], heads, rel, query, met_ref[...], *outs)


def gradient_shapes(features, edges):
    return [jax.ShapeDtypeStruct((features, edges), bf16)] * 4


def gradient_specs(features, span):
    return [across(features, span)] * 4


def cost(units, span, features, rows):
    return pl.CostEstimate(flops=units * span, bytes_accessed=1 << 16, transcendentals=0)


def query_call(ids, left, table, span):
    edges = ids.shape[1]
    features, rows = left.shape
    return pl.pallas_call(
        query_kernel,
        grid=(edges // span,),
        in_specs=[across(4, span), whole(left.shape), whole(table.shape)],
        out_specs=[across(features, span)] * 3,
        out_shape=[
            jax.ShapeDtypeStruct((features, edges), bf16),
            jax.ShapeDtypeStruct((features, edges), f32),
            jax.ShapeDtypeStruct((features, edges), bf16),
        ],
        compiler_params=params(),
        cost_estimate=cost(2, edges, features, rows),
        name="queries",
    )(ids, left, table)


def gradient_call(ids, heads, rel, query, right, span):
    features, edges = heads.shape
    return pl.pallas_call(
        gradient_kernel,
        grid=(edges // span,),
        in_specs=[across(4, span)] + [across(features, span)] * 3 + [whole(right.shape)],
        out_specs=gradient_specs(features, span),
        out_shape=gradient_shapes(features, edges),
        compiler_params=params(),
        cost_estimate=cost(3, edges, features, right.shape[1]),
        name="gradients",
    )(ids, heads, rel, query, right)


def paired_call(home, ids, own, met, passed, table, span):
    edges = ids.shape[1]
    features, rows = own.shape
    return pl.pallas_call(
        paired_kernel,
        grid=(edges // span,),
        in_specs=[pl.BlockSpec(memory_space=pltpu.SMEM), across(4, span)]
        + [whole(own.shape)] * 3
        + [whole(table.shape)],
        out_specs=gradient_specs(features, span),
        out_shape=gradient_shapes(features, edges),
        scratch_shapes=[pltpu.VMEM(own.shape, bf16)],
        compiler_params=params(),
        cost_estimate=cost(5, edges, features, rows),
        name="paired",
    )(home, ids, own, met, passed, table)


def scatter_kernel(chunk, lines, has_start, *refs):
    first = pl.program_id(0) * chunk
    n_pairs = len(lines)
    ins = 2 * n_pairs + has_start
    total = None
    for k, line in enumerate(lines):
        part = dot_nt(one_hot(refs[2 * k][line : line + 1, :], chunk, first), refs[2 * k + 1][...])
        total = part if total is None else total + part
    if has_start:
        total = total + refs[2 * n_pairs][...].astype(f32)
    for out_ref in refs[ins:]:
        out_ref[...] = total.astype(out_ref.dtype)


def scatter_call(pairs, rows, dtypes, start=None, chunk=512):
    features = pairs[0][2].shape[0]
    chunk = min(chunk, rows)
    operands, specs = [], []
    for ids, _, vectors in pairs:
        operands += [ids, vectors]
        specs += [whole(ids.shape), whole(vectors.shape)]
    down = pl.BlockSpec((chunk, features), lambda s: (s, 0))
    if start is not None:
        operands.append(start)
        specs.append(down)

    def kernel(*refs):
        scatter_kernel(chunk, [line for _, line, _ in pairs], start is not None, *refs)

    outs = pl.pallas_call(
        kernel,
        grid=(rows // chunk,),
        in_specs=specs,
        out_specs=[down] * len(dtypes),
        out_shape=[jax.ShapeDtypeStruct((rows, features), dtype) for dtype in dtypes],
        compiler_params=params(),
        cost_estimate=cost(1, sum(v.shape[1] for _, _, v in pairs), features, rows),
        name="scatter",
    )(*operands)
    return outs[0] if len(outs) == 1 else outs


def update_kernel(home_ref, entity_ref, acc_ref, left_ref, outer_ref, inner_ref, back_ref, new_ref, acc_new_ref):
    rows = entity_ref.shape[0]
    grad = left_ref[...] + outer_ref[...].astype(f32) + back_ref[...].astype(f32)
    grad = grad + jnp.where(home_ref[0] == 1, inner_ref[...].astype(f32), 0.0)
    mean = jnp.mean(grad * grad, axis=1, keepdims=True)
    acc_new = acc_ref[...] + jnp.broadcast_to(mean, (rows, 128)).T[:1]
    acc_new_ref[...] = acc_new
    scale = learn_rate / jnp.sqrt(jnp.broadcast_to(acc_new, (128, rows)).T[:, :1])
    new_ref[...] = (entity_ref[...].astype(f32) - scale * grad).astype(bf16)


def update_call(home, entity, acc, left, outer, inner, back, chunk=512):
    rows, features = entity.shape
    down = pl.BlockSpec((chunk, features), lambda s: (s, 0))
    line = pl.BlockSpec((1, chunk), lambda s: (0, s))
    new, acc_new = pl.pallas_call(
        update_kernel,
        grid=(rows // chunk,),
        in_specs=[pl.BlockSpec(memory_space=pltpu.SMEM), down, line, down, down, down, down],
        out_specs=[down, line],
        out_shape=[jax.ShapeDtypeStruct((rows, features), bf16), jax.ShapeDtypeStruct((1, rows), f32)],
        compiler_params=params(),
        cost_estimate=pl.CostEstimate(flops=10 * rows * features, bytes_accessed=10 << 20, transcendentals=rows),
        name="update",
    )(home, entity, acc.reshape(1, rows), left, outer, inner, back)
    return new, acc_new.reshape(rows)


def relation_mine(partial, axes):
    devices = 1
    for axis in axes:
        devices *= lax.axis_size(axis)
    rows, features = partial.shape
    return lax.all_to_all(partial.reshape(devices, rows // devices, features), axes, 0, 0, tiled=True)


def relation_spread(pieces, axes):
    mine = jnp.sum(pieces.astype(f32), axis=0).astype(bf16)
    spread = jnp.broadcast_to(mine[None], pieces.shape)
    return lax.all_to_all(spread, axes, 0, 0, tiled=True).reshape(-1, pieces.shape[2]).astype(f32)


def body(entity, entity_acc, relation, rel_acc, edge_src, edge_rel, edge_dst, negatives):
    axes = ("grp", "dom")
    groups, doms = lax.axis_size("grp"), lax.axis_size("dom")
    half = doms // 2
    rows, features = entity.shape
    n_rel = relation.shape[0]
    spans, span = negatives.shape[2:]
    edges = spans * span
    step = max(128, 8 * groups * doms)
    rel_rows = -(-n_rel // step) * step

    places = [(g, d) for g in range(groups) for d in range(doms)]

    def is_home(g, d):
        return g % 2 == d // half

    def send(block, to, only=lambda g, d: True):
        route = []
        for g, d in places:
            if only(g, d):
                h, e = to(g, d)
                route.append((g * doms + d, h % groups * doms + e % doms))
        return lax.ppermute(block, axes, route)

    def guest(g, d):
        return not is_home(g, d)

    def meeting(g, d):
        return (g ^ 1, d) if is_home(g, d) else (g, d + half)

    def parting(g, d):
        return (g, d + half) if is_home(g, d) else (g ^ 1, d)

    def neighbour(g, d):
        return g ^ 1, d

    home = (lax.axis_index("grp") % 2 == lax.axis_index("dom") // half).astype(jnp.int32).reshape(1)

    def id_lines(bucket):
        lines = [a[0, bucket].reshape(edges) for a in (edge_src, edge_rel, edge_dst, negatives)]
        return jnp.stack(lines)

    own = entity.T
    met = send(own, meeting)
    outer = send(own, lambda g, d: (g + 1, d))
    ids_two, ids_one = id_lines(1), id_lines(0)
    sent_ids = send(ids_one, lambda g, d: (g ^ 1, d + half), guest)
    ids_one = jnp.where(home == 1, ids_one, sent_ids)

    padded = jnp.pad(relation, ((0, rel_rows - n_rel), (0, 0))).T
    high = lax.reduce_precision(padded, 8, 7)
    table = jnp.concatenate([high.astype(bf16), (padded - high).astype(bf16)], axis=0)

    heads, rel, query = query_call(ids_two, own, table, span)
    dl_two, dt_two, dc_two, dp_two = gradient_call(ids_two, heads, rel, query, outer, span)
    met, dp_two = lax.optimization_barrier((met, dp_two))
    passed = send(met, neighbour, is_home)
    rel_part = scatter_call([(ids_two, 1, dp_two)], rel_rows, [f32])
    passed, rel_part = lax.optimization_barrier((passed, rel_part))
    dl_one, dt_one, dc_one, dp_one = paired_call(home, ids_one, own, met, passed, table, span)
    rel_sum = scatter_call([(ids_one, 1, dp_one)], rel_rows, [bf16], rel_part)
    rel_mine = relation_mine(rel_sum, axes)
    dl_one, rel_sum = lax.optimization_barrier((dl_one, rel_sum))
    left_one = scatter_call([(ids_one, 0, dl_one)], rows, [bf16])
    guest_left = send(left_one, neighbour, guest)
    d_right_one = scatter_call([(ids_one, 2, dt_one), (ids_one, 3, dc_one)], rows, [bf16], guest_left)
    back = send(d_right_one, parting)
    d_right_one, dt_two = lax.optimization_barrier((d_right_one, dt_two))
    d_right_two = scatter_call([(ids_two, 2, dt_two), (ids_two, 3, dc_two)], rows, [bf16])
    back_outer = send(d_right_two, lambda g, d: (g - 1, d))
    d_right_two, dl_two = lax.optimization_barrier((d_right_two, dl_two))
    left_two = scatter_call([(ids_two, 0, dl_two)], rows, [f32])
    entity_new, entity_acc_new = update_call(home, entity, entity_acc, left_two, back_outer, left_one, back)
    rel_total = relation_spread(rel_mine, axes)[:n_rel]
    rel_acc_new = rel_acc + jnp.mean(rel_total * rel_total, axis=1)
    relation_new = relation - learn_rate * rel_total / jnp.sqrt(rel_acc_new)[:, None]
    return (entity_new, entity_acc_new, relation_new, rel_acc_new)


def solution(mesh):
    return jax.shard_map(
        body,
        mesh=mesh,
        in_specs=(
            P(("grp", "dom"), None),
            P(("grp", "dom")),
            P(),
            P(),
            P(("grp", "dom"), None, None),
            P(("grp", "dom"), None, None),
            P(("grp", "dom"), None, None),
            P(("grp", "dom"), None, None, None),
        ),
        out_specs=(P(("grp", "dom"), None), P(("grp", "dom")), P(), P()),
        check_vma=False,
    )
```

time: 179 us -> 154 us (0.86)
  the two profiles are of different devices: /device:TPU:0 before, /device:TPU:24 now
where the time goes in v1:
time: 154 us; the launch traced here: 153 us
  Pallas kernels  92.2 us (60%)
  waiting for transfers between devices  26.2 us (17%)
  starting transfers between devices  21.5 us (14%)
  local copies, waits for them, and re-layouts  6.4 us (4%)
  other arithmetic  5.92 us (4%)
    pallas_call x6, Pallas kernels, scatter_call(): pl.pallas_call(kernel, grid=(rows // chunk,), in_specs=specs, out_specs=[...  36.7 us
    pallas_call x1, Pallas kernels, paired_call(): pl.pallas_call(paired_kernel, grid=(edges // span,), in_specs=[pl.BlockSp...  24 us
    ppermute x7, waiting for transfers between devices, send(): return lax.ppermute(block, axes, route)  20.1 us
    pallas_call x1, Pallas kernels, gradient_call(): pl.pallas_call(gradient_kernel, grid=(edges // span,), in_specs=[across(4...  16.5 us
    ppermute x7, starting transfers between devices, send(): return lax.ppermute(block, axes, route)  10.2 us
    pallas_call x1, Pallas kernels, query_call(): pl.pallas_call(query_kernel, grid=(edges // span,), in_specs=[across(4, s...  9.95 us
    all_to_all x1, waiting for transfers between devices, relation_mine(): lax.all_to_all(partial.reshape(devices, rows // devices, features), axes,...  6.09 us
    all_to_all x1, starting transfers between devices, relation_spread(): lax.all_to_all(spread, axes, 0, 0, tiled=True).reshape(-1, pieces.shape[2])  5.89 us
  transfers between devices with their start and end apart: 9, of which 5 were waited for; matrix products, arithmetic and copies ran while one was open for 5% of the time, Pallas kernels for 38%

profile of v1, /device:TPU:24, one launch (start us, length us, event | category | flops | bytes accessed | tf_op | source)
XLA Modules:
  0.0 153.2 jit_solution(14389593514516736397)
XLA Ops:
  0.6 0.0 copy-start.6
  0.6 1.5 copy.12
  2.1 0.1 collective-permute-start.2
  2.2 0.4 collective-permute-start.1
  2.6 0.0 copy-done.6
  2.6 0.0 copy-start.8
  2.6 0.0 copy-start.9
  2.7 1.6 %copy.13 = f32[1000,256]{0,1:T(8,128)S(1)} copy(f32[1000,256]{1,0:T(8,128)} %param.10) | data formatting | bytes 2048000 | tf_op args[2]
  4.2 0.0 copy-start.7
  4.2 0.2 reduce-precision_convert_fusion
  4.4 0.0 copy-done.8
  4.4 0.0 copy-done.9
  4.5 0.5 copy-done.7
  5.0 0.1 pad_add_fusion.ids_ref.refs_0_.refs_2_
  5.0 1.0 pad_maximum_fusion.table_ref
  6.1 10.0 %queries.1 = (bf16[256,3072]{1,0:T(8,128)(2,1)}, f32[256,3072]{1,0:T(8,128)}, bf16[256,3072]{1,0:T(8,128)(2,1)}) custom-call(s32[4,3072]{1,0:T(4,128)S(1)} %pad_add_fusion.ids_ref.refs_0_.refs_2_, bf16[256,2048]{1,0:T(8,128)(2,1)S(1)} %bitcast.26, bf16[512,1024]{1,0:T(8,128)(2,1)} %pad_maximum_fusion.table_ref), custom_call_target="tpu_custom_call" | custom-call | flops 6144 | bytes 65536 | tf_op jit(solution)/shard_map/queries/pallas_call | solution.py:130
  16.0 0.4 collective-permute-done.2.right_ref
  16.4 16.5 %gradients.1 = (bf16[256,3072]{1,0:T(8,128)(2,1)}, bf16[256,3072]{1,0:T(8,128)(2,1)}, bf16[256,3072]{1,0:T(8,128)(2,1)}, bf16[256,3072]{1,0:T(8,128)(2,1)}) custom-call(s32[4,3072]{1,0:T(4,128)S(1)} %pad_add_fusion.ids_ref.refs_0_.refs_2_, bf16[256,3072]{1,0:T(8,128)(2,1)} %get-tuple-element.24.heads_ref, f32[256,3072]{1,0:T(8,128)} %get-tuple-element.25.rel_ref, ...), custom_call_target="tpu_custom_call" | custom-call | flops 9216 | bytes 65536 | tf_op jit(solution)/shard_map/gradients/pallas_call | solution.py:148
  32.9 0.0 collective-permute-done.1.met_ref
  32.9 1.3 collective-permute-start.3
  34.2 0.1 pad_add_fusion.1
  34.3 5.0 %collective-permute-start = (s32[4,3072]{1,0:T(4,128)S(1)}, s32[4,3072]{1,0:T(4,128)S(1)}, u32[]{:S(2)}, u32[]{:S(2)}) collective-permute-start(s32[4,3072]{1,0:T(4,128)S(1)} %pad_add_fusion.1), channel_id=1, source_target_pairs={{4,8},{5,9},{6,10},{7,11},{8,4},{9,5},{10,6},{11,7},{20,24},{21,25... | collective-permute-start | bytes 147464 | tf_op jit(solution)/shard_map/ppermute | solution.py:284
  39.3 2.1 %collective-permute-done = s32[4,3072]{1,0:T(4,128)S(1)} collective-permute-done((s32[4,3072]{1,0:T(4,128)S(1)}, s32[4,3072]{1,0:T(4,128)S(1)}, u32[]{:S(2)}, u32[]{:S(2)}) %collective-permute-start) | collective-permute-done | bytes 49184 | tf_op jit(solution)/shard_map/ppermute | solution.py:284
  41.4 0.1 broadcast_select_fusion.ids_ref.refs_0_.refs_2_
  41.5 3.5 %scatter.6.refs_2_ = f32[1024,256]{1,0:T(8,128)S(1)} custom-call(s32[4,3072]{1,0:T(4,128)S(1)} %pad_add_fusion.ids_ref.refs_0_.refs_2_, bf16[256,3072]{1,0:T(8,128)(2,1)} %get-tuple-element.29.refs_1_), custom_call_target="tpu_custom_call" | custom-call | flops 3072 | bytes 65536 | tf_op jit(solution)/shard_map/scatter/pallas_call | solution.py:207
  45.0 0.0 collective-permute-done.3.passed_ref
  45.0 0.0 copy-start.4
  45.0 1.0 copy-done.4
  46.0 24.0 %paired.1 = (bf16[256,3072]{1,0:T(8,128)(2,1)}, bf16[256,3072]{1,0:T(8,128)(2,1)}, bf16[256,3072]{1,0:T(8,128)(2,1)}, bf16[256,3072]{1,0:T(8,128)(2,1)}) custom-call(s32[1]{0:T(128)} %bitcast.home_ref, s32[4,3072]{1,0:T(4,128)S(1)} %broadcast_select_fusion.ids_ref.refs_0_.refs_2_, bf16[256,2048]{1,0:T(8,128)(2,1)S(1)} %bitcast.27, ...), custom_call_target="tpu_custom_call" | custom-call | flops 15360 | bytes 65536 | tf_op jit(solution)/shard_map/paired/pallas_call | solution.py:163
  70.0 4.2 %scatter.7 = bf16[1024,256]{1,0:T(8,128)(2,1)} custom-call(s32[4,3072]{1,0:T(4,128)S(1)} %broadcast_select_fusion.ids_ref.refs_0_.refs_2_, bf16[256,3072]{1,0:T(8,128)(2,1)} %get-tuple-element.34.refs_1_, f32[1024,256]{1,0:T(8,128)S(1)} %scatter.6.refs_2_), custom_call_target="tpu_custom_call" | custom-call | flops 3072 | bytes 65536 | tf_op jit(solution)/shard_map/scatter/pallas_call | solution.py:207
  74.1 5.4 %all-to-all-start = ((bf16[32,32,256]{2,1,0:T(8,128)(2,1)}), bf16[32,32,256]{2,1,0:T(8,128)(2,1)S(1)}, u32[]{:S(2)}, u32[]{:S(2)}) async-start(bf16[32,32,256]{2,1,0:T(8,128)(2,1)} %bitcast.14), calls=%async_computation | async-start | bytes 1048576 | tf_op jit(solution)/shard_map/all_to_all | solution.py:253
  79.6 5.5 %scatter.8.inner_ref = bf16[2048,256]{1,0:T(8,128)(2,1)S(1)} custom-call(s32[4,3072]{1,0:T(4,128)S(1)} %broadcast_select_fusion.ids_ref.refs_0_.refs_2_, bf16[256,3072]{1,0:T(8,128)(2,1)} %get-tuple-element.36.refs_1_), custom_call_target="tpu_custom_call" | custom-call | flops 3072 | bytes 65536 | tf_op jit(solution)/shard_map/scatter/pallas_call | solution.py:207
  85.1 0.0 copy-start.1
  85.1 2.1 %collective-permute-start.4 = (bf16[2048,256]{1,0:T(8,128)(2,1)S(1)}, bf16[2048,256]{1,0:T(8,128)(2,1)S(1)}, u32[]{:S(2)}, u32[]{:S(2)}) collective-permute-start(bf16[2048,256]{1,0:T(8,128)(2,1)S(1)} %scatter.8.inner_ref), channel_id=1, source_target_pairs={{4,12},{5,13},{6,14},{7,15},{8,0},{9,1},{10,2},{11,3},{20,28},{21,... | collective-permute-start | bytes 3145736 | tf_op jit(solution)/shard_map/ppermute | solution.py:284
  87.2 6.1 %all-to-all-done = bf16[32,32,256]{2,1,0:T(8,128)(2,1)S(1)} async-done(((bf16[32,32,256]{2,1,0:T(8,128)(2,1)}), bf16[32,32,256]{2,1,0:T(8,128)(2,1)S(1)}, u32[]{:S(2)}, u32[]{:S(2)}) %all-to-all-start) | async-done | bytes 524320 | tf_op jit(solution)/shard_map/all_to_all | solution.py:253
  93.3 0.1 reduce_sum.21
  93.4 0.9 broadcast_in_dim.16
  94.3 5.9 %all-to-all-start.1 = ((bf16[32,32,256]{2,1,0:T(8,128)(2,1)}), bf16[32,32,256]{2,1,0:T(8,128)(2,1)}, u32[]{:S(2)}, u32[]{:S(2)}) async-start(bf16[32,32,256]{2,1,0:T(8,128)(2,1)} %broadcast_in_dim.16), calls=%async_computation.1 | async-start | bytes 1048576 | tf_op jit(solution)/shard_map/all_to_all | solution.py:259
  100.2 0.0 collective-permute-done.4.refs_4_
  100.2 0.0 copy-start.5
  100.2 1.0 copy-done.5
  101.1 9.3 %scatter.9 = bf16[2048,256]{1,0:T(8,128)(2,1)S(1)} custom-call(s32[4,3072]{1,0:T(4,128)S(1)} %broadcast_select_fusion.ids_ref.refs_0_.refs_2_, bf16[256,3072]{1,0:T(8,128)(2,1)} %get-tuple-element.31.refs_1_, s32[4,3072]{1,0:T(4,128)S(1)} %broadcast_select_fusion.ids_ref.refs_0_.refs_2_, bf16[256,3072]{1,0:T(8,128)(2,1)} %get-tuple-element.32.refs_3_, ...), custom_call_target="tpu_custom_call" | custom-call | flops 6144 | bytes 65536 | tf_op jit(solution)/shard_map/scatter/pallas_call | solution.py:207
  110.5 0.0 copy-done.1
  110.5 0.0 copy-start.2
  110.5 9.3 %scatter.10 = bf16[2048,256]{1,0:T(8,128)(2,1)S(1)} custom-call(s32[4,3072]{1,0:T(4,128)S(1)} %pad_add_fusion.ids_ref.refs_0_.refs_2_, bf16[256,3072]{1,0:T(8,128)(2,1)} %get-tuple-element.38.refs_1_, s32[4,3072]{1,0:T(4,128)S(1)} %pad_add_fusion.ids_ref.refs_0_.refs_2_, bf16[256,3072]{1,0:T(8,128)(2,1)} %get-tuple-element.39.refs_3_), custom_call_target="tpu_custom_call" | custom-call | flops 6144 | bytes 65536 | tf_op jit(solution)/shard_map/scatter/pallas_call | solution.py:207
  119.8 1.3 collective-permute-start.5
  121.1 0.0 collective-permute-start.6
  121.1 0.0 copy-done.2
  121.1 0.0 copy-start.10
  121.1 4.9 %scatter.11.left_ref = f32[2048,256]{1,0:T(8,128)} custom-call(s32[4,3072]{1,0:T(4,128)S(1)} %pad_add_fusion.ids_ref.refs_0_.refs_2_, bf16[256,3072]{1,0:T(8,128)(2,1)S(1)} %copy-done.2), custom_call_target="tpu_custom_call" | custom-call | flops 3072 | bytes 65536 | tf_op jit(solution)/shard_map/scatter/pallas_call | solution.py:207
  126.0 0.0 copy-start
  126.0 0.0 copy-start.3
  126.0 0.0 all-to-all-done.1
  126.0 1.3 fusion.3
  127.4 0.0 copy-done.10
  127.4 0.6 fusion.4
  128.0 2.5 %fusion.2 = f32[1000,256]{1,0:T(8,128)} fusion(f32[1000,256]{1,0:T(8,128)} %param.10, f32[1000]{0:T(1024)S(1)} %get-tuple-element.44, bf16[1024,256]{1,0:T(8,128)(2,1)} %bitcast.15), kind=kLoop, calls=%fused_computation.7 | loop fusion | flops 1024000 | bytes 2564000 | tf_op jit(solution)/shard_map/sub | solution.py:337
  130.5 3.0 %collective-permute-done.5.outer_ref = bf16[2048,256]{1,0:T(8,128)(2,1)} collective-permute-done((bf16[2048,256]{1,0:T(8,128)(2,1)S(1)}, bf16[2048,256]{1,0:T(8,128)(2,1)}, u32[]{:S(2)}, u32[]{:S(2)}) %collective-permute-start.5) | collective-permute-done | bytes 1048608 | tf_op jit(solution)/shard_map/ppermute | solution.py:284
  133.4 14.6 %collective-permute-done.6.back_ref = bf16[2048,256]{1,0:T(8,128)(2,1)} collective-permute-done((bf16[2048,256]{1,0:T(8,128)(2,1)S(1)}, bf16[2048,256]{1,0:T(8,128)(2,1)}, u32[]{:S(2)}, u32[]{:S(2)}) %collective-permute-start.6) | collective-permute-done | bytes 1048608 | tf_op jit(solution)/shard_map/ppermute | solution.py:284
  148.1 0.0 copy-done
  148.1 0.0 copy-done.3
  148.1 5.1 %update.1 = (bf16[2048,256]{1,0:T(8,128)(2,1)}, f32[1,2048]{1,0:T(1,128)}) custom-call(s32[1]{0:T(128)} %bitcast.home_ref, bf16[2048,256]{1,0:T(8,128)(2,1)S(1)} %copy-done, f32[1,2048]{1,0:T(1,128)S(1)} %bitcast.28, f32[2048,256]{1,0:T(8,128)} %scatter.11.left_ref, bf16[2048,256]{1,0:T(8,128)(2,1)} %collective-permute-done.5.outer_ref, ...), custom_call_target="tpu_custom_call" | custom-call | flops 5242880 | bytes 10485760 | tf_op jit(solution)/shard_map/update/pallas_call | solution.py:235
  (3 shorter events, 0.1 us)
Async XLA Ops:
  0.6 2.0 %copy-start.6 = (s32[1,2,6,512]{3,1,2,0:T(2,128)S(1)}, s32[1,2,6,512]{3,1,2,0:T(2,128)}, u32[]{:S(2)}) copy-start(s32[1,2,6,512]{3,1,2,0:T(2,128)} %param.15) | copy-start | bytes 73732
  2.1 14.3 %collective-permute-start.2 = (bf16[256,2048]{1,0:T(8,128)(2,1)S(1)}, bf16[256,2048]{1,0:T(8,128)(2,1)S(1)}, u32[]{:S(2)}, u32[]{:S(2)}) collective-permute-start(bf16[256,2048]{1,0:T(8,128)(2,1)S(1)} %bitcast.24), channel_id=1, source_target_pairs={{0,8},{1,9},{2,10},{3,11},{4,12},{5,13},{6,14},{7,15},{8,16},{9,17... | collective-permute-start | bytes 3145736 | tf_op jit(solution)/shard_map/ppermute | solution.py:284
  2.2 30.7 %collective-permute-start.1 = (bf16[256,2048]{1,0:T(8,128)(2,1)S(1)}, bf16[256,2048]{1,0:T(8,128)(2,1)}, u32[]{:S(2)}, u32[]{:S(2)}) collective-permute-start(bf16[256,2048]{1,0:T(8,128)(2,1)S(1)} %bitcast.25), channel_id=1, source_target_pairs={{0,8},{1,9},{2,10},{3,11},{4,0},{5,1},{6,2},{7,3},{8,12},{9,13},{1... | collective-permute-start | bytes 3145736 | tf_op jit(solution)/shard_map/ppermute | solution.py:284
  2.6 1.8 %copy-start.8 = (s32[1,2,3072]{2,1,0:T(2,128)S(1)}, s32[1,2,3072]{2,1,0:T(2,128)}, u32[]{:S(2)}) copy-start(s32[1,2,3072]{2,1,0:T(2,128)} %param.14) | copy-start | bytes 73732
  2.6 1.8 %copy-start.9 = (s32[1,2,3072]{2,1,0:T(2,128)S(1)}, s32[1,2,3072]{2,1,0:T(2,128)}, u32[]{:S(2)}) copy-start(s32[1,2,3072]{2,1,0:T(2,128)} %param.13) | copy-start | bytes 73732
  4.2 0.7 copy-start.7
  32.9 12.1 %collective-permute-start.3 = (bf16[256,2048]{1,0:T(8,128)(2,1)}, bf16[256,2048]{1,0:T(8,128)(2,1)S(1)}, u32[]{:S(2)}, u32[]{:S(2)}) collective-permute-start(bf16[256,2048]{1,0:T(8,128)(2,1)} %collective-permute-done.1.met_ref), channel_id=1, source_target_pairs={{0,8},{1,9},{2,10},{3,11},{12,4},{13,5},{14,6},{15,7},{16,24},{17,... | collective-permute-start | bytes 3145736 | tf_op jit(solution)/shard_map/ppermute | solution.py:284
  34.3 7.2 %collective-permute-start = (s32[4,3072]{1,0:T(4,128)S(1)}, s32[4,3072]{1,0:T(4,128)S(1)}, u32[]{:S(2)}, u32[]{:S(2)}) collective-permute-start(s32[4,3072]{1,0:T(4,128)S(1)} %pad_add_fusion.1), channel_id=1, source_target_pairs={{4,8},{5,9},{6,10},{7,11},{8,4},{9,5},{10,6},{11,7},{20,24},{21,25... | collective-permute-start | bytes 147464 | tf_op jit(solution)/shard_map/ppermute | solution.py:284
  45.0 1.0 copy-start.4
  74.1 19.2 %all-to-all-start = ((bf16[32,32,256]{2,1,0:T(8,128)(2,1)}), bf16[32,32,256]{2,1,0:T(8,128)(2,1)S(1)}, u32[]{:S(2)}, u32[]{:S(2)}) async-start(bf16[32,32,256]{2,1,0:T(8,128)(2,1)} %bitcast.14), calls=%async_computation | async-start | bytes 1048576 | tf_op jit(solution)/shard_map/all_to_all | solution.py:253
  85.1 25.4 %copy-start.1 = (bf16[2048,256]{1,0:T(8,128)(2,1)}, bf16[2048,256]{1,0:T(8,128)(2,1)S(1)}, u32[]{:S(2)}) copy-start(bf16[2048,256]{1,0:T(8,128)(2,1)S(1)} %scatter.8.inner_ref) | copy-start | bytes 3145732
  85.1 15.1 %collective-permute-start.4 = (bf16[2048,256]{1,0:T(8,128)(2,1)S(1)}, bf16[2048,256]{1,0:T(8,128)(2,1)S(1)}, u32[]{:S(2)}, u32[]{:S(2)}) collective-permute-start(bf16[2048,256]{1,0:T(8,128)(2,1)S(1)} %scatter.8.inner_ref), channel_id=1, source_target_pairs={{4,12},{5,13},{6,14},{7,15},{8,0},{9,1},{10,2},{11,3},{20,28},{21,... | collective-permute-start | bytes 3145736 | tf_op jit(solution)/shard_map/ppermute | solution.py:284
  94.3 31.8 %all-to-all-start.1 = ((bf16[32,32,256]{2,1,0:T(8,128)(2,1)}), bf16[32,32,256]{2,1,0:T(8,128)(2,1)}, u32[]{:S(2)}, u32[]{:S(2)}) async-start(bf16[32,32,256]{2,1,0:T(8,128)(2,1)} %broadcast_in_dim.16), calls=%async_computation.1 | async-start | bytes 1048576 | tf_op jit(solution)/shard_map/all_to_all | solution.py:259
  100.2 1.0 copy-start.5
  110.5 10.7 %copy-start.2 = (bf16[256,3072]{1,0:T(8,128)(2,1)S(1)}, bf16[256,3072]{1,0:T(8,128)(2,1)}, u32[]{:S(2)}) copy-start(bf16[256,3072]{1,0:T(8,128)(2,1)} %get-tuple-element.41.refs_1_) | copy-start | bytes 4718596
  119.8 13.6 %collective-permute-start.5 = (bf16[2048,256]{1,0:T(8,128)(2,1)S(1)}, bf16[2048,256]{1,0:T(8,128)(2,1)}, u32[]{:S(2)}, u32[]{:S(2)}) collective-permute-start(bf16[2048,256]{1,0:T(8,128)(2,1)S(1)} %scatter.10), channel_id=1, source_target_pairs={{0,24},{1,25},{2,26},{3,27},{4,28},{5,29},{6,30},{7,31},{8,0},{9,1... | collective-permute-start | bytes 3145736 | tf_op jit(solution)/shard_map/ppermute | solution.py:284
  121.1 27.0 %collective-permute-start.6 = (bf16[2048,256]{1,0:T(8,128)(2,1)S(1)}, bf16[2048,256]{1,0:T(8,128)(2,1)}, u32[]{:S(2)}, u32[]{:S(2)}) collective-permute-start(bf16[2048,256]{1,0:T(8,128)(2,1)S(1)} %scatter.9), channel_id=1, source_target_pairs={{0,4},{1,5},{2,6},{3,7},{4,12},{5,13},{6,14},{7,15},{8,0},{9,1},{1... | collective-permute-start | bytes 3145736 | tf_op jit(solution)/shard_map/ppermute | solution.py:284
  121.1 6.2 %copy-start.10 = (f32[1000]{0:T(1024)S(1)}, f32[1000]{0:T(1024)}, u32[]{:S(2)}) copy-start(f32[1000]{0:T(1024)} %param.11) | copy-start | bytes 12004
  126.0 22.1 %copy-start = (bf16[2048,256]{1,0:T(8,128)(2,1)S(1)}, bf16[2048,256]{1,0:T(8,128)(2,1)}, u32[]{:S(2)}) copy-start(bf16[2048,256]{1,0:T(8,128)(2,1)} %entity_ref.1) | copy-start | bytes 3145732
  126.0 22.1 %copy-start.3 = (f32[2048]{0:T(1024)S(1)}, f32[2048]{0:T(1024)}, u32[]{:S(2)}) copy-start(f32[2048]{0:T(1024)} %param.9) | copy-start | bytes 24580

commit v2 on v1

v2 whole, which is shorter than its diff:
```python
import jax
import jax.numpy as jnp
from jax import lax
from jax.experimental import pallas as pl
from jax.experimental.pallas import tpu as pltpu
from jax.sharding import PartitionSpec as P

learn_rate = 0.3
bf16 = jnp.bfloat16
f32 = jnp.float32
VMEM_LIMIT = 52 << 20


def dot_nn(a, b):
    return jnp.dot(a, b, preferred_element_type=f32)


def dot_nt(a, b):
    return lax.dot_general(a, b, (((1,), (1,)), ((), ())), preferred_element_type=f32)


def one_hot(ids, rows, first=0):
    shape = (rows, ids.shape[1])
    match = (ids - first).astype(jnp.int16) == lax.broadcasted_iota(jnp.int16, shape, 0)
    return jnp.where(match, jnp.ones((), bf16), jnp.zeros((), bf16))


def whole(shape):
    return pl.BlockSpec(shape, lambda s: (0,) * len(shape))


def across(height, width):
    return pl.BlockSpec((height, width), lambda s: (0, s))


def params():
    return pltpu.CompilerParams(dimension_semantics=("arbitrary",), vmem_limit_bytes=VMEM_LIMIT)


def halves(a):
    middle = a.shape[0] // 2
    return a[:middle], a[middle:]


def make_query(source, rel_ids, left, rel_table):
    features, rows = left.shape
    heads = dot_nn(left, one_hot(source, rows))
    both = dot_nn(rel_table, one_hot(rel_ids, rel_table.shape[1]))
    rel = both[:features] + both[features:]
    h_re, h_im = halves(heads)
    r_re, r_im = halves(rel)
    query = jnp.concatenate([h_re * r_re - h_im * r_im, h_re * r_im + h_im * r_re], 0)
    return heads, rel, query.astype(bf16)


def make_gradients(targets, negatives, heads, rel, query, right, heads_out, tails_out, cands_out, rels_out):
    rows = right.shape[1]
    tails = dot_nn(right, one_hot(targets, rows))
    cands = dot_nn(right, one_hot(negatives, rows)).astype(bf16)
    query32 = query.astype(f32)
    positive = jnp.sum(query32 * tails, axis=0, keepdims=True)
    scores = dot_nn(cands.T, query)
    peak = jnp.maximum(jnp.max(scores, axis=0, keepdims=True), positive)
    expd = jnp.exp(scores - peak)
    own = jnp.exp(positive - peak)
    inverse = 1.0 / (own + jnp.sum(expd, axis=0, keepdims=True))
    shares = (expd * inverse).astype(bf16)
    coefficient = own * inverse - 1.0
    tails_out[...] = (coefficient * query32).astype(bf16)
    cands_out[...] = dot_nt(query, shares).astype(bf16)
    grad = coefficient * tails + dot_nn(cands, shares)
    g_re, g_im = halves(grad)
    r_re, r_im = halves(rel)
    h_re, h_im = halves(heads)
    heads_out[...] = jnp.concatenate(
        [g_re * r_re + g_im * r_im, g_im * r_re - g_re * r_im], 0
    ).astype(bf16)
    rels_out[...] = jnp.concatenate(
        [g_re * h_re + g_im * h_im, g_im * h_re - g_re * h_im], 0
    ).astype(bf16)


def lines_kernel(source_ref, rel_ref, target_ref, negatives_ref, *outs):
    _, spans, _, span = negatives_ref.shape
    for bucket, out_ref in enumerate(outs):
        for line, ref in enumerate((source_ref, rel_ref, target_ref)):
            out_ref[line : line + 1] = ref[0, bucket : bucket + 1]
        for s in range(spans):
            out_ref[3:4, s * span : (s + 1) * span] = negatives_ref[0, s, bucket : bucket + 1]


def lines_call(*arrays):
    edges = arrays[0].shape[2]
    return pl.pallas_call(
        lines_kernel,
        in_specs=[pl.BlockSpec(memory_space=pltpu.VMEM)] * 4,
        out_specs=[pl.BlockSpec(memory_space=pltpu.VMEM)] * 2,
        out_shape=[jax.ShapeDtypeStruct((4, edges), jnp.int32)] * 2,
        cost_estimate=cost(1, 1, 1, 1),
        name="lines",
    )(*arrays)


def query_kernel(ids_ref, own_ref, relation_ref, heads_ref, rel_ref, query_ref, table_ref, left, padded):
    @pl.when(pl.program_id(0) == 0)
    def _():
        n_rel, features = relation_ref.shape
        left[...] = own_ref[...].T
        padded[:n_rel] = relation_ref[...]
        padded[n_rel:] = jnp.zeros((padded.shape[0] - n_rel, features), f32)
        across_rel = padded[...].T
        high = across_rel.astype(bf16)
        table_ref[:features] = high
        table_ref[features:] = (across_rel - high.astype(f32)).astype(bf16)

    ids = ids_ref[...]
    heads, rel, query = make_query(ids[0:1], ids[1:2], left[...], table_ref[...])
    heads_ref[...] = heads.astype(bf16)
    rel_ref[...] = rel
    query_ref[...] = query


def gradient_kernel(ids_ref, heads_ref, rel_ref, query_ref, partner_ref, *rest):
    *outs, right = rest

    @pl.when(pl.program_id(0) == 0)
    def _():
        right[...] = partner_ref[...].T

    ids = ids_ref[...]
    heads = heads_ref[...].astype(f32)
    make_gradients(ids[2:3], ids[3:4], heads, rel_ref[...], query_ref[...], right[...], *outs)


def paired_kernel(home_ref, ids_ref, own_ref, met_ref, passed_ref, table_ref, *rest):
    *outs, left, right = rest

    @pl.when(pl.program_id(0) == 0)
    def _():
        right[...] = met_ref[...].T

        @pl.when(home_ref[0] == 1)
        def _():
            left[...] = own_ref[...].T

        @pl.when(home_ref[0] == 0)
        def _():
            left[...] = passed_ref[...].T

    ids = ids_ref[...]
    heads, rel, query = make_query(ids[0:1], ids[1:2], left[...], table_ref[...])
    make_gradients(ids[2:3], ids[3:4], heads, rel, query, right[...], *outs)


def gradient_shapes(features, edges):
    return [jax.ShapeDtypeStruct((features, edges), bf16)] * 4


def gradient_specs(features, span):
    return [across(features, span)] * 4


def cost(units, span, features, rows):
    return pl.CostEstimate(flops=1 << 40, bytes_accessed=1 << 32, transcendentals=0)


def query_call(ids, own, relation, rel_rows, span):
    edges = ids.shape[1]
    rows, features = own.shape
    return pl.pallas_call(
        query_kernel,
        grid=(edges // span,),
        in_specs=[across(4, span), whole(own.shape), whole(relation.shape)],
        out_specs=[across(features, span)] * 3 + [whole((2 * features, rel_rows))],
        out_shape=[
            jax.ShapeDtypeStruct((features, edges), bf16),
            jax.ShapeDtypeStruct((features, edges), f32),
            jax.ShapeDtypeStruct((features, edges), bf16),
            jax.ShapeDtypeStruct((2 * features, rel_rows), bf16),
        ],
        scratch_shapes=[pltpu.VMEM((features, rows), bf16), pltpu.VMEM((rel_rows, features), f32)],
        compiler_params=params(),
        cost_estimate=cost(2, edges, features, rows),
        name="queries",
    )(ids, own, relation)


def gradient_call(ids, heads, rel, query, partner, span):
    features, edges = heads.shape
    rows = partner.shape[0]
    return pl.pallas_call(
        gradient_kernel,
        grid=(edges // span,),
        in_specs=[across(4, span)] + [across(features, span)] * 3 + [whole(partner.shape)],
        out_specs=gradient_specs(features, span),
        out_shape=gradient_shapes(features, edges),
        scratch_shapes=[pltpu.VMEM((features, rows), bf16)],
        compiler_params=params(),
        cost_estimate=cost(3, edges, features, rows),
        name="gradients",
    )(ids, heads, rel, query, partner)


def paired_call(home, ids, own, met, passed, table, span):
    edges = ids.shape[1]
    rows, features = own.shape
    return pl.pallas_call(
        paired_kernel,
        grid=(edges // span,),
        in_specs=[pl.BlockSpec(memory_space=pltpu.SMEM), across(4, span)]
        + [whole(own.shape)] * 3
        + [whole(table.shape)],
        out_specs=gradient_specs(features, span),
        out_shape=gradient_shapes(features, edges),
        scratch_shapes=[pltpu.VMEM((features, rows), bf16)] * 2,
        compiler_params=params(),
        cost_estimate=cost(5, edges, features, rows),
        name="paired",
    )(home, ids, own, met, passed, table)


def scatter_kernel(chunk, lines, n_starts, *refs):
    first = pl.program_id(0) * chunk
    n_pairs = len(lines)
    ins = 2 * n_pairs + n_starts
    total = None
    for k, line in enumerate(lines):
        part = dot_nt(one_hot(refs[2 * k][line : line + 1, :], chunk, first), refs[2 * k + 1][...])
        total = part if total is None else total + part
    for start in refs[2 * n_pairs : ins]:
        total = total + start[...].astype(f32)
    for out_ref in refs[ins:]:
        out_ref[...] = total.astype(out_ref.dtype)


def scatter_call(pairs, rows, dtypes, starts=(), chunk=512):
    features = pairs[0][2].shape[0]
    chunk = min(chunk, rows)
    operands, specs = [], []
    for ids, _, vectors in pairs:
        operands += [ids, vectors]
        specs += [whole(ids.shape), whole(vectors.shape)]
    down = pl.BlockSpec((chunk, features), lambda s: (s, 0))
    for start in starts:
        operands.append(start)
        specs.append(down)

    def kernel(*refs):
        scatter_kernel(chunk, [line for _, line, _ in pairs], len(starts), *refs)

    outs = pl.pallas_call(
        kernel,
        grid=(rows // chunk,),
        in_specs=specs,
        out_specs=[down] * len(dtypes),
        out_shape=[jax.ShapeDtypeStruct((rows, features), dtype) for dtype in dtypes],
        compiler_params=params(),
        cost_estimate=cost(1, sum(v.shape[1] for _, _, v in pairs), features, rows),
        name="scatter",
    )(*operands)
    return outs[0] if len(outs) == 1 else outs


def adagrad_lines(grad, acc):
    rows = grad.shape[0]
    mean = jnp.mean(grad * grad, axis=1, keepdims=True)
    acc_new = acc + jnp.broadcast_to(mean, (rows, 128)).T[:1]
    scale = learn_rate / jnp.sqrt(acc_new)
    return acc_new, jnp.broadcast_to(scale, (128, rows)).T[:, :1]


def update_kernel(home_ref, entity_ref, acc_ref, local_ref, outer_ref, inner_ref, back_ref, new_ref, acc_new_ref):
    grad = local_ref[...] + outer_ref[...].astype(f32) + back_ref[...].astype(f32)
    grad = grad + jnp.where(home_ref[0] == 1, inner_ref[...].astype(f32), 0.0)
    acc_new, scale = adagrad_lines(grad, acc_ref[...])
    acc_new_ref[...] = acc_new
    new_ref[...] = (entity_ref[...].astype(f32) - scale * grad).astype(bf16)


def update_call(home, entity, acc, local, outer, inner, back, chunk=512):
    rows, features = entity.shape
    down = pl.BlockSpec((chunk, features), lambda s: (s, 0))
    line = pl.BlockSpec((1, chunk), lambda s: (0, s))
    new, acc_new = pl.pallas_call(
        update_kernel,
        grid=(rows // chunk,),
        in_specs=[pl.BlockSpec(memory_space=pltpu.SMEM), down, line, down, down, down, down],
        out_specs=[down, line],
        out_shape=[jax.ShapeDtypeStruct((rows, features), bf16), jax.ShapeDtypeStruct((1, rows), f32)],
        compiler_params=params(),
        cost_estimate=cost(1, rows, features, rows),
        name="update",
    )(home, entity, acc.reshape(1, rows), local, outer, inner, back)
    return new, acc_new.reshape(rows)


def relation_kernel(relation_ref, acc_ref, total_ref, new_ref, acc_new_ref):
    n_rel = relation_ref.shape[0]
    total = total_ref[...].astype(f32)
    acc_new, scale = adagrad_lines(total, acc_ref[...])
    acc_new_ref[...] = acc_new[:, :n_rel]
    new_ref[...] = relation_ref[...] - scale[:n_rel] * total[:n_rel]


def relation_call(relation, acc, total):
    n_rel = relation.shape[0]
    line = jnp.pad(acc.reshape(1, n_rel), ((0, 0), (0, total.shape[0] - n_rel)), constant_values=1.0)
    new, acc_new = pl.pallas_call(
        relation_kernel,
        in_specs=[pl.BlockSpec(memory_space=pltpu.VMEM)] * 3,
        out_specs=[pl.BlockSpec(memory_space=pltpu.VMEM)] * 2,
        out_shape=[jax.ShapeDtypeStruct(relation.shape, f32), jax.ShapeDtypeStruct((1, n_rel), f32)],
        compiler_params=pltpu.CompilerParams(vmem_limit_bytes=VMEM_LIMIT),
        cost_estimate=cost(1, 1, 1, 1),
        name="relation",
    )(relation, line, total)
    return new, acc_new.reshape(n_rel)


def shares_kernel(pieces_ref, out_ref):
    share = jnp.sum(pieces_ref[...].astype(f32), axis=0).astype(bf16)
    for k in range(out_ref.shape[0]):
        out_ref[k] = share


def shares_call(pieces, copies):
    return pl.pallas_call(
        shares_kernel,
        in_specs=[pl.BlockSpec(memory_space=pltpu.VMEM)],
        out_specs=pl.BlockSpec(memory_space=pltpu.VMEM),
        out_shape=jax.ShapeDtypeStruct((copies,) + pieces.shape[1:], bf16),
        cost_estimate=cost(1, 1, 1, 1),
        name="shares",
    )(pieces)


def body(entity, entity_acc, relation, rel_acc, edge_src, edge_rel, edge_dst, negatives):
    axes = ("grp", "dom")
    groups, doms = lax.axis_size("grp"), lax.axis_size("dom")
    half = doms // 2
    rows, features = entity.shape
    n_rel = relation.shape[0]
    spans, span = negatives.shape[2:]
    edges = spans * span
    step = max(128, 8 * groups * doms)
    rel_rows = -(-n_rel // step) * step

    places = [(g, d) for g in range(groups) for d in range(doms)]

    def is_home(g, d):
        return g % 2 == d // half

    def send(block, to, only=lambda g, d: True):
        route = []
        for g, d in places:
            if only(g, d):
                h, e = to(g, d)
                route.append((g * doms + d, h % groups * doms + e % doms))
        return lax.ppermute(block, axes, route)

    def guest(g, d):
        return not is_home(g, d)

    def meeting(g, d):
        return (g ^ 1, d) if is_home(g, d) else (g, d + half)

    def parting(g, d):
        return (g, d + half) if is_home(g, d) else (g ^ 1, d)

    def neighbour(g, d):
        return g ^ 1, d

    home = (lax.axis_index("grp") % 2 == lax.axis_index("dom") // half).astype(jnp.int32).reshape(1)

    ids_one, ids_two = lines_call(edge_src, edge_rel, edge_dst, negatives.transpose(0, 2, 1, 3))
    met = send(entity, meeting)
    outer = send(entity, lambda g, d: (g + 1, d))
    heads, rel, query, table = query_call(ids_two, entity, relation, rel_rows, span)
    dl_two, dt_two, dc_two, dp_two = gradient_call(ids_two, heads, rel, query, outer, span)
    met, ids_one, dt_two = lax.optimization_barrier((met, ids_one, dt_two))
    passed = send(met, neighbour, is_home)
    sent_ids = send(ids_one, lambda g, d: (g ^ 1, d + half), guest)
    rel_part = scatter_call([(ids_two, 1, dp_two)], rel_rows, [f32])
    passed, sent_ids, rel_part = lax.optimization_barrier((passed, sent_ids, rel_part))
    ids_one = jnp.where(home == 1, ids_one, sent_ids)
    dl_one, dt_one, dc_one, dp_one = paired_call(home, ids_one, entity, met, passed, table, span)

    left_one = scatter_call([(ids_one, 0, dl_one)], rows, [bf16])
    guest_left = send(left_one, neighbour, guest)
    d_right_one = scatter_call([(ids_one, 2, dt_one), (ids_one, 3, dc_one)], rows, [bf16], [guest_left])
    back = send(d_right_one, parting)
    d_right_one, dp_one, dt_two, dl_two = lax.optimization_barrier((d_right_one, dp_one, dt_two, dl_two))

    planes = [[g * doms + q + x for g in range(groups) for x in range(2)] for q in range(0, doms, 2)]
    stacks = [[g * doms + q + x for q in range(0, doms, 2)] for g in range(groups) for x in range(2)]

    def exchange(pieces, sets):
        return lax.all_to_all(pieces, axes, 0, 0, axis_index_groups=sets, tiled=True)

    rel_sum = scatter_call([(ids_one, 1, dp_one)], rel_rows, [bf16], [rel_part])
    shares = exchange(rel_sum.reshape(2 * groups, -1, features), planes)
    rel_sum, dt_two = lax.optimization_barrier((rel_sum, dt_two))
    d_right_two = scatter_call([(ids_two, 2, dt_two), (ids_two, 3, dc_two)], rows, [bf16])
    back_outer = send(d_right_two, lambda g, d: (g - 1, d))
    shares, d_right_two = lax.optimization_barrier((shares, d_right_two))
    shares = exchange(shares_call(shares, len(stacks[0])), stacks)
    d_right_two, dl_two = lax.optimization_barrier((d_right_two, dl_two))
    local = scatter_call([(ids_two, 0, dl_two)], rows, [f32])
    shares, local = lax.optimization_barrier((shares, local))
    total = exchange(shares_call(shares, len(planes[0])), planes).reshape(rel_rows, features)
    entity_new, entity_acc_new = update_call(home, entity, entity_acc, local, back_outer, left_one, back)
    relation_new, rel_acc_new = relation_call(relation, rel_acc, total)
    return (entity_new, entity_acc_new, relation_new, rel_acc_new)


def solution(mesh):
    return jax.shard_map(
        body,
        mesh=mesh,
        in_specs=(
            P(("grp", "dom"), None),
            P(("grp", "dom")),
            P(),
            P(),
            P(("grp", "dom"), None, None),
            P(("grp", "dom"), None, None),
            P(("grp", "dom"), None, None),
            P(("grp", "dom"), None, None, None),
        ),
        out_specs=(P(("grp", "dom"), None), P(("grp", "dom")), P(), P()),
        check_vma=False,
    )
```

time: 154 us -> 145 us (0.942)
  the two profiles are of different devices: /device:TPU:24 before, /device:TPU:0 now
where the time goes in v2:
time: 145 us; the launch traced here: 144 us
  Pallas kernels  104 us (72%)
  starting transfers between devices  25.5 us (18%)
  waiting for transfers between devices  10.8 us (7%)
  local copies, waits for them, and re-layouts  1.81 us (1%)
    pallas_call x6, Pallas kernels, scatter_call(): pl.pallas_call(kernel, grid=(rows // chunk,), in_specs=specs, out_specs=[...  38.1 us
    pallas_call x1, Pallas kernels, paired_call(): pl.pallas_call(paired_kernel, grid=(edges // span,), in_specs=[pl.BlockSp...  24.7 us
    pallas_call x1, Pallas kernels, gradient_call(): pl.pallas_call(gradient_kernel, grid=(edges // span,), in_specs=[across(4...  17.4 us
    ppermute x7, starting transfers between devices, send(): return lax.ppermute(block, axes, route)  13 us
    all_to_all x3, starting transfers between devices, exchange(): lax.all_to_all(pieces, axes, 0, 0, axis_index_groups=sets, tiled=True)  12.5 us
    pallas_call x1, Pallas kernels, query_call(): pl.pallas_call(query_kernel, grid=(edges // span,), in_specs=[across(4, s...  10.6 us
    all_to_all x3, waiting for transfers between devices, exchange(): lax.all_to_all(pieces, axes, 0, 0, axis_index_groups=sets, tiled=True)  7.55 us
    pallas_call x1, Pallas kernels, update_call(): pl.pallas_call(update_kernel, grid=(rows // chunk,), in_specs=[pl.BlockSp...  5.19 us
  transfers between devices with their start and end apart: 10, of which 3 were waited for; matrix products, arithmetic and copies ran while one was open for 0% of the time, Pallas kernels for 42%

profile of v2, /device:TPU:0, one launch (start us, length us, event | category | flops | bytes accessed | tf_op | source)
XLA Modules:
  0.0 143.7 jit_solution(15002918403502415794)
XLA Ops:
  0.6 0.5 collective-permute-start.1
  1.1 2.6 %collective-permute-start = (bf16[2048,256]{1,0:T(8,128)(2,1)}, bf16[2048,256]{1,0:T(8,128)(2,1)}, u32[]{:S(2)}, u32[]{:S(2)}) collective-permute-start(bf16[2048,256]{1,0:T(8,128)(2,1)} %entity_ref.1), channel_id=1, source_target_pairs={{0,8},{1,9},{2,10},{3,11},{4,0},{5,1},{6,2},{7,3},{8,12},{9,13},{1... | collective-permute-start | bytes 3145736 | tf_op jit(solution)/shard_map/ppermute | solution.py:359
  3.8 0.0 copy-start.3
  3.8 1.5 %lines.1 = (s32[4,3072]{1,0:T(4,128)}, s32[4,3072]{1,0:T(4,128)}) custom-call(s32[1,2,3072]{2,1,0:T(2,128)} %source_ref.1, s32[1,2,3072]{2,1,0:T(2,128)} %rel_ref.1, s32[1,2,3072]{2,1,0:T(2,128)} %target_ref.1, s32[1,6,2,512]{3,2,1,0:T(2,128)} %bitcast.11), custom_call_target="tpu_custom_call" | custom-call | flops 1099511627776 | bytes 4294967296 | tf_op jit(solution)/shard_map/lines/pallas_call | solution.py:94
  5.3 0.0 copy-done.3
  5.3 0.0 copy-start.7
  5.3 0.8 copy-done.7
  6.1 0.0 copy-start.8
  6.1 10.6 %queries.1 = (bf16[256,3072]{1,0:T(8,128)(2,1)}, f32[256,3072]{1,0:T(8,128)}, bf16[256,3072]{1,0:T(8,128)(2,1)}, bf16[512,1024]{1,0:T(8,128)(2,1)}) custom-call(s32[4,3072]{1,0:T(4,128)S(1)} %copy-done.7, bf16[2048,256]{1,0:T(8,128)(2,1)} %entity_ref.1, f32[1000,256]{1,0:T(8,128)S(1)} %copy-done.3), custom_call_target="tpu_custom_call" | custom-call | flops 1099511627776 | bytes 4294967296 | tf_op jit(solution)/shard_map/queries/pallas_call | solution.py:170
  16.7 0.0 collective-permute-done.1.partner_ref
  16.7 0.0 copy-done.8
  16.7 17.4 %gradients.1 = (bf16[256,3072]{1,0:T(8,128)(2,1)}, bf16[256,3072]{1,0:T(8,128)(2,1)}, bf16[256,3072]{1,0:T(8,128)(2,1)}, bf16[256,3072]{1,0:T(8,128)(2,1)}) custom-call(s32[4,3072]{1,0:T(4,128)S(1)} %copy-done.8, bf16[256,3072]{1,0:T(8,128)(2,1)} %get-tuple-element.37.heads_ref, f32[256,3072]{1,0:T(8,128)} %get-tuple-element.38.rel_ref, ...), custom_call_target="tpu_custom_call" | custom-call | flops 1099511627776 | bytes 4294967296 | tf_op jit(solution)/shard_map/gradients/pallas_call | solution.py:191
  34.1 0.0 collective-permute-done.met_ref
  34.1 5.2 %collective-permute-start.2 = (bf16[2048,256]{1,0:T(8,128)(2,1)}, bf16[2048,256]{1,0:T(8,128)(2,1)}, u32[]{:S(2)}, u32[]{:S(2)}) collective-permute-start(bf16[2048,256]{1,0:T(8,128)(2,1)} %collective-permute-done.met_ref), channel_id=1, source_target_pairs={{0,8},{1,9},{2,10},{3,11},{12,4},{13,5},{14,6},{15,7},{16,24},{17,... | collective-permute-start | bytes 3145736 | tf_op jit(solution)/shard_map/ppermute | solution.py:359
  39.3 1.3 collective-permute-start.3
  40.5 0.0 copy-start
  40.5 3.5 %scatter.6.refs_2_ = f32[1024,256]{1,0:T(8,128)S(1)} custom-call(s32[4,3072]{1,0:T(4,128)S(1)} %copy-done.8, bf16[256,3072]{1,0:T(8,128)(2,1)} %get-tuple-element.43.refs_1_), custom_call_target="tpu_custom_call" | custom-call | flops 1099511627776 | bytes 4294967296 | tf_op jit(solution)/shard_map/scatter/pallas_call | solution.py:251
  44.1 0.0 collective-permute-done.3
  44.1 0.0 collective-permute-done.2.passed_ref
  44.1 0.8 broadcast_select_fusion.ids_ref.refs_0_.refs_2_
  44.9 0.0 copy-done
  44.9 24.7 %paired.1 = (bf16[256,3072]{1,0:T(8,128)(2,1)}, bf16[256,3072]{1,0:T(8,128)(2,1)}, bf16[256,3072]{1,0:T(8,128)(2,1)}, bf16[256,3072]{1,0:T(8,128)(2,1)}) custom-call(s32[1]{0:T(128)} %bitcast.home_ref, s32[4,3072]{1,0:T(4,128)S(1)} %broadcast_select_fusion.ids_ref.refs_0_.refs_2_, bf16[2048,256]{1,0:T(8,128)(2,1)S(1)} %copy-done, ...), custom_call_target="tpu_custom_call" | custom-call | flops 1099511627776 | bytes 4294967296 | tf_op jit(solution)/shard_map/paired/pallas_call | solution.py:207
  69.7 0.0 copy-start.10
  69.7 5.5 %scatter.7.inner_ref = bf16[2048,256]{1,0:T(8,128)(2,1)S(1)} custom-call(s32[4,3072]{1,0:T(4,128)S(1)} %broadcast_select_fusion.ids_ref.refs_0_.refs_2_, bf16[256,3072]{1,0:T(8,128)(2,1)} %get-tuple-element.49.refs_1_), custom_call_target="tpu_custom_call" | custom-call | flops 1099511627776 | bytes 4294967296 | tf_op jit(solution)/shard_map/scatter/pallas_call | solution.py:251
  75.2 0.0 copy-start.2
  75.2 1.3 collective-permute-start.4
  76.5 0.0 copy-done.2
  76.5 0.0 copy-done.10
  76.5 3.2 %collective-permute-done.4.refs_4_ = bf16[2048,256]{1,0:T(8,128)(2,1)S(1)} collective-permute-done((bf16[2048,256]{1,0:T(8,128)(2,1)S(1)}, bf16[2048,256]{1,0:T(8,128)(2,1)S(1)}, u32[]{:S(2)}, u32[]{:S(2)}) %collective-permute-start.4) | collective-permute-done | bytes 1048608 | tf_op jit(solution)/shard_map/ppermute | solution.py:359
  79.7 0.0 copy-start.11
  79.7 1.0 copy-done.11
  80.7 10.0 %scatter.8 = bf16[2048,256]{1,0:T(8,128)(2,1)} custom-call(s32[4,3072]{1,0:T(4,128)S(1)} %broadcast_select_fusion.ids_ref.refs_0_.refs_2_, bf16[256,3072]{1,0:T(8,128)(2,1)} %get-tuple-element.47.refs_1_, s32[4,3072]{1,0:T(4,128)S(1)} %broadcast_select_fusion.ids_ref.refs_0_.refs_2_, bf16[256,3072]{1,0:T(8,128)(2,1)} %get-tuple-element.48.refs_3_, ...), custom_call_target="tpu_custom_call" | custom-call | flops 1099511627776 | bytes 4294967296 | tf_op jit(solution)/shard_map/scatter/pallas_call | solution.py:251
  90.7 0.6 collective-permute-start.6
  91.4 4.1 %scatter.9 = bf16[1024,256]{1,0:T(8,128)(2,1)} custom-call(s32[4,3072]{1,0:T(4,128)S(1)} %broadcast_select_fusion.ids_ref.refs_0_.refs_2_, bf16[256,3072]{1,0:T(8,128)(2,1)} %get-tuple-element.53.refs_1_, f32[1024,256]{1,0:T(8,128)S(1)} %scatter.6.refs_2_), custom_call_target="tpu_custom_call" | custom-call | flops 1099511627776 | bytes 4294967296 | tf_op jit(solution)/shard_map/scatter/pallas_call | solution.py:251
  95.5 4.3 %all-to-all-start = ((bf16[8,128,256]{2,1,0:T(8,128)(2,1)}), bf16[8,128,256]{2,1,0:T(8,128)(2,1)}, u32[]{:S(2)}, u32[]{:S(2)}) async-start(bf16[8,128,256]{2,1,0:T(8,128)(2,1)} %bitcast.4), calls=%async_computation | async-start | bytes 1048576 | tf_op jit(solution)/shard_map/all_to_all | solution.py:398
  99.9 9.9 %scatter.10 = bf16[2048,256]{1,0:T(8,128)(2,1)} custom-call(s32[4,3072]{1,0:T(4,128)S(1)} %copy-done.8, bf16[256,3072]{1,0:T(8,128)(2,1)} %get-tuple-element.56.refs_1_, s32[4,3072]{1,0:T(4,128)S(1)} %copy-done.8, bf16[256,3072]{1,0:T(8,128)(2,1)} %get-tuple-element.57.refs_3_), custom_call_target="tpu_custom_call" | custom-call | flops 1099511627776 | bytes 4294967296 | tf_op jit(solution)/shard_map/scatter/pallas_call | solution.py:251
  109.8 1.5 %collective-permute-start.5 = (bf16[2048,256]{1,0:T(8,128)(2,1)}, bf16[2048,256]{1,0:T(8,128)(2,1)}, u32[]{:S(2)}, u32[]{:S(2)}) collective-permute-start(bf16[2048,256]{1,0:T(8,128)(2,1)} %scatter.10), channel_id=1, source_target_pairs={{0,24},{1,25},{2,26},{3,27},{4,28},{5,29},{6,30},{7,31},{8,0},{9,1... | collective-permute-start | bytes 3145736 | tf_op jit(solution)/shard_map/ppermute | solution.py:359
  111.3 0.0 all-to-all-done.pieces_ref
  111.3 0.0 copy-start.6
  111.3 0.0 copy-start.9
  111.3 1.9 %shares.2 = bf16[4,128,256]{2,1,0:T(8,128)(2,1)} custom-call(bf16[8,128,256]{2,1,0:T(8,128)(2,1)} %all-to-all-done.pieces_ref), custom_call_target="tpu_custom_call" | custom-call | flops 1099511627776 | bytes 4294967296 | tf_op jit(solution)/shard_map/shares/pallas_call | solution.py:327
  113.2 4.0 %all-to-all-start.1 = ((bf16[4,128,256]{2,1,0:T(8,128)(2,1)}), bf16[4,128,256]{2,1,0:T(8,128)(2,1)}, u32[]{:S(2)}, u32[]{:S(2)}) async-start(bf16[4,128,256]{2,1,0:T(8,128)(2,1)} %shares.2), calls=%async_computation.1 | async-start | bytes 524288 | tf_op jit(solution)/shard_map/all_to_all | solution.py:398
  117.3 0.0 copy-done.6
  117.3 0.0 copy-done.9
  117.3 4.9 %scatter.11.local_ref = f32[2048,256]{1,0:T(8,128)} custom-call(s32[4,3072]{1,0:T(4,128)S(1)} %copy-done.9, bf16[256,3072]{1,0:T(8,128)(2,1)S(1)} %copy-done.6), custom_call_target="tpu_custom_call" | custom-call | flops 1099511627776 | bytes 4294967296 | tf_op jit(solution)/shard_map/scatter/pallas_call | solution.py:251
  122.2 3.5 %all-to-all-done.1.pieces_ref = bf16[4,128,256]{2,1,0:T(8,128)(2,1)} async-done(((bf16[4,128,256]{2,1,0:T(8,128)(2,1)}), bf16[4,128,256]{2,1,0:T(8,128)(2,1)}, u32[]{:S(2)}, u32[]{:S(2)}) %all-to-all-start.1) | async-done | bytes 262176 | tf_op jit(solution)/shard_map/all_to_all | solution.py:398
  125.7 0.0 copy-start.1
  125.7 0.0 copy-start.5
  125.7 1.9 %shares.3 = bf16[8,128,256]{2,1,0:T(8,128)(2,1)} custom-call(bf16[4,128,256]{2,1,0:T(8,128)(2,1)} %all-to-all-done.1.pieces_ref), custom_call_target="tpu_custom_call" | custom-call | flops 1099511627776 | bytes 4294967296 | tf_op jit(solution)/shard_map/shares/pallas_call | solution.py:327
  127.6 4.2 %all-to-all-start.2 = ((bf16[8,128,256]{2,1,0:T(8,128)(2,1)}), bf16[8,128,256]{2,1,0:T(8,128)(2,1)}, u32[]{:S(2)}, u32[]{:S(2)}) async-start(bf16[8,128,256]{2,1,0:T(8,128)(2,1)} %shares.3), calls=%async_computation.2 | async-start | bytes 1048576 | tf_op jit(solution)/shard_map/all_to_all | solution.py:398
  131.7 0.0 collective-permute-done.5.outer_ref
  131.7 0.0 collective-permute-done.6.back_ref
  131.7 0.0 copy-done.1
  131.8 0.0 copy-done.5
  131.8 0.0 copy-start.4
  131.8 5.2 %update.1 = (bf16[2048,256]{1,0:T(8,128)(2,1)}, f32[1,2048]{1,0:T(1,128)}) custom-call(s32[1]{0:T(128)} %bitcast.home_ref, bf16[2048,256]{1,0:T(8,128)(2,1)S(1)} %copy-done.1, f32[1,2048]{1,0:T(1,128)S(1)} %bitcast.9, f32[2048,256]{1,0:T(8,128)} %scatter.11.local_ref, bf16[2048,256]{1,0:T(8,128)(2,1)} %collective-permute-done.5.outer_ref, ...), custom_call_target="tpu_custom_call" | custom-call | flops 1099511627776 | bytes 4294967296 | tf_op jit(solution)/shard_map/update/pallas_call | solution.py:284
  137.0 4.0 %all-to-all-done.2 = bf16[8,128,256]{2,1,0:T(8,128)(2,1)} async-done(((bf16[8,128,256]{2,1,0:T(8,128)(2,1)}), bf16[8,128,256]{2,1,0:T(8,128)(2,1)}, u32[]{:S(2)}, u32[]{:S(2)}) %all-to-all-start.2) | async-done | bytes 524320 | tf_op jit(solution)/shard_map/all_to_all | solution.py:398
  141.0 0.0 copy-done.4
  141.0 2.7 %relation.1 = (f32[1000,256]{1,0:T(8,128)}, f32[1,1000]{1,0:T(1,128)}) custom-call(f32[1000,256]{1,0:T(8,128)S(1)} %copy-done.4, f32[1,1024]{1,0:T(1,128)S(1)} %pad.4.acc_ref, bf16[1024,256]{1,0:T(8,128)(2,1)} %bitcast.7.total_ref), custom_call_target="tpu_custom_call" | custom-call | flops 1099511627776 | bytes 4294967296 | tf_op jit(solution)/shard_map/relation/pallas_call | solution.py:308
  (1 shorter events, 0.0 us)
Async XLA Ops:
  0.6 16.1 %collective-permute-start.1 = (bf16[2048,256]{1,0:T(8,128)(2,1)}, bf16[2048,256]{1,0:T(8,128)(2,1)}, u32[]{:S(2)}, u32[]{:S(2)}) collective-permute-start(bf16[2048,256]{1,0:T(8,128)(2,1)} %entity_ref.1), channel_id=1, source_target_pairs={{0,8},{1,9},{2,10},{3,11},{4,12},{5,13},{6,14},{7,15},{8,16},{9,17... | collective-permute-start | bytes 3145736 | tf_op jit(solution)/shard_map/ppermute | solution.py:359
  1.1 32.9 %collective-permute-start = (bf16[2048,256]{1,0:T(8,128)(2,1)}, bf16[2048,256]{1,0:T(8,128)(2,1)}, u32[]{:S(2)}, u32[]{:S(2)}) collective-permute-start(bf16[2048,256]{1,0:T(8,128)(2,1)} %entity_ref.1), channel_id=1, source_target_pairs={{0,8},{1,9},{2,10},{3,11},{4,0},{5,1},{6,2},{7,3},{8,12},{9,13},{1... | collective-permute-start | bytes 3145736 | tf_op jit(solution)/shard_map/ppermute | solution.py:359
  3.8 1.5 %copy-start.3 = (f32[1000,256]{1,0:T(8,128)S(1)}, f32[1000,256]{1,0:T(8,128)}, u32[]{:S(2)}) copy-start(f32[1000,256]{1,0:T(8,128)} %relation_ref.3) | copy-start | bytes 3072004
  5.3 0.8 copy-start.7
  6.1 10.6 %copy-start.8 = (s32[4,3072]{1,0:T(4,128)S(1)}, s32[4,3072]{1,0:T(4,128)}, u32[]{:S(2)}) copy-start(s32[4,3072]{1,0:T(4,128)} %get-tuple-element.36.ids_ref.refs_0_.refs_2_) | copy-start | bytes 147460
  34.1 10.0 %collective-permute-start.2 = (bf16[2048,256]{1,0:T(8,128)(2,1)}, bf16[2048,256]{1,0:T(8,128)(2,1)}, u32[]{:S(2)}, u32[]{:S(2)}) collective-permute-start(bf16[2048,256]{1,0:T(8,128)(2,1)} %collective-permute-done.met_ref), channel_id=1, source_target_pairs={{0,8},{1,9},{2,10},{3,11},{12,4},{13,5},{14,6},{15,7},{16,24},{17,... | collective-permute-start | bytes 3145736 | tf_op jit(solution)/shard_map/ppermute | solution.py:359
  39.3 4.8 %collective-permute-start.3 = (s32[4,3072]{1,0:T(4,128)}, s32[4,3072]{1,0:T(4,128)}, u32[]{:S(2)}, u32[]{:S(2)}) collective-permute-start(s32[4,3072]{1,0:T(4,128)} %get-tuple-element.41), channel_id=1, source_target_pairs={{4,8},{5,9},{6,10},{7,11},{8,4},{9,5},{10,6},{11,7},{20,24},{21,25... | collective-permute-start | bytes 147464 | tf_op jit(solution)/shard_map/ppermute | solution.py:359
  40.5 4.4 %copy-start = (bf16[2048,256]{1,0:T(8,128)(2,1)S(1)}, bf16[2048,256]{1,0:T(8,128)(2,1)}, u32[]{:S(2)}) copy-start(bf16[2048,256]{1,0:T(8,128)(2,1)} %entity_ref.1) | copy-start | bytes 3145732
  69.7 6.8 %copy-start.10 = (f32[1000]{0:T(1024)S(1)}, f32[1000]{0:T(1024)}, u32[]{:S(2)}) copy-start(f32[1000]{0:T(1024)} %param.11) | copy-start | bytes 12004
  75.2 1.3 copy-start.2
  75.2 4.6 %collective-permute-start.4 = (bf16[2048,256]{1,0:T(8,128)(2,1)S(1)}, bf16[2048,256]{1,0:T(8,128)(2,1)S(1)}, u32[]{:S(2)}, u32[]{:S(2)}) collective-permute-start(bf16[2048,256]{1,0:T(8,128)(2,1)S(1)} %scatter.7.inner_ref), channel_id=1, source_target_pairs={{4,12},{5,13},{6,14},{7,15},{8,0},{9,1},{10,2},{11,3},{20,28},{21,... | collective-permute-start | bytes 3145736 | tf_op jit(solution)/shard_map/ppermute | solution.py:359
  79.7 1.0 copy-start.11
  90.7 41.0 %collective-permute-start.6 = (bf16[2048,256]{1,0:T(8,128)(2,1)}, bf16[2048,256]{1,0:T(8,128)(2,1)}, u32[]{:S(2)}, u32[]{:S(2)}) collective-permute-start(bf16[2048,256]{1,0:T(8,128)(2,1)} %scatter.8), channel_id=1, source_target_pairs={{0,4},{1,5},{2,6},{3,7},{4,12},{5,13},{6,14},{7,15},{8,0},{9,1},{1... | collective-permute-start | bytes 3145736 | tf_op jit(solution)/shard_map/ppermute | solution.py:359
  95.5 15.7 %all-to-all-start = ((bf16[8,128,256]{2,1,0:T(8,128)(2,1)}), bf16[8,128,256]{2,1,0:T(8,128)(2,1)}, u32[]{:S(2)}, u32[]{:S(2)}) async-start(bf16[8,128,256]{2,1,0:T(8,128)(2,1)} %bitcast.4), calls=%async_computation | async-start | bytes 1048576 | tf_op jit(solution)/shard_map/all_to_all | solution.py:398
  109.8 21.9 %collective-permute-start.5 = (bf16[2048,256]{1,0:T(8,128)(2,1)}, bf16[2048,256]{1,0:T(8,128)(2,1)}, u32[]{:S(2)}, u32[]{:S(2)}) collective-permute-start(bf16[2048,256]{1,0:T(8,128)(2,1)} %scatter.10), channel_id=1, source_target_pairs={{0,24},{1,25},{2,26},{3,27},{4,28},{5,29},{6,30},{7,31},{8,0},{9,1... | collective-permute-start | bytes 3145736 | tf_op jit(solution)/shard_map/ppermute | solution.py:359
  111.3 6.0 %copy-start.6 = (bf16[256,3072]{1,0:T(8,128)(2,1)S(1)}, bf16[256,3072]{1,0:T(8,128)(2,1)}, u32[]{:S(2)}) copy-start(bf16[256,3072]{1,0:T(8,128)(2,1)} %get-tuple-element.59.refs_1_) | copy-start | bytes 4718596
  111.3 6.0 %copy-start.9 = (s32[4,3072]{1,0:T(4,128)S(1)}, s32[4,3072]{1,0:T(4,128)}, u32[]{:S(2)}) copy-start(s32[4,3072]{1,0:T(4,128)} %get-tuple-element.36.ids_ref.refs_0_.refs_2_) | copy-start | bytes 147460
  113.2 12.5 %all-to-all-start.1 = ((bf16[4,128,256]{2,1,0:T(8,128)(2,1)}), bf16[4,128,256]{2,1,0:T(8,128)(2,1)}, u32[]{:S(2)}, u32[]{:S(2)}) async-start(bf16[4,128,256]{2,1,0:T(8,128)(2,1)} %shares.2), calls=%async_computation.1 | async-start | bytes 524288 | tf_op jit(solution)/shard_map/all_to_all | solution.py:398
  125.7 6.1 %copy-start.1 = (bf16[2048,256]{1,0:T(8,128)(2,1)S(1)}, bf16[2048,256]{1,0:T(8,128)(2,1)}, u32[]{:S(2)}) copy-start(bf16[2048,256]{1,0:T(8,128)(2,1)} %entity_ref.1) | copy-start | bytes 3145732
  125.7 6.1 %copy-start.5 = (f32[2048]{0:T(1024)S(1)}, f32[2048]{0:T(1024)}, u32[]{:S(2)}) copy-start(f32[2048]{0:T(1024)} %param.9) | copy-start | bytes 24580
  127.6 13.4 %all-to-all-start.2 = ((bf16[8,128,256]{2,1,0:T(8,128)(2,1)}), bf16[8,128,256]{2,1,0:T(8,128)(2,1)}, u32[]{:S(2)}, u32[]{:S(2)}) async-start(bf16[8,128,256]{2,1,0:T(8,128)(2,1)} %shares.3), calls=%async_computation.2 | async-start | bytes 1048576 | tf_op jit(solution)/shard_map/all_to_all | solution.py:398
  131.8 9.2 %copy-start.4 = (f32[1000,256]{1,0:T(8,128)S(1)}, f32[1000,256]{1,0:T(8,128)}, u32[]{:S(2)}) copy-start(f32[1000,256]{1,0:T(8,128)} %relation_ref.3) | copy-start | bytes 3072004

commit v3 on v2

--- a/solution.py
+++ b/solution.py
@@ -1,3 +1,5 @@
+import functools
+
 import jax
 import jax.numpy as jnp
 from jax import lax
@@ -53,10 +55,19 @@
     return heads, rel, query.astype(bf16)
 
 
-def make_gradients(targets, negatives, heads, rel, query, right, heads_out, tails_out, cands_out, rels_out):
+def make_gradients(span, targets, negatives, heads, rel, query, right, outs):
+    width = query.shape[1]
     rows = right.shape[1]
-    tails = dot_nn(right, one_hot(targets, rows))
-    cands = dot_nn(right, one_hot(negatives, rows)).astype(bf16)
+    picked = dot_nn(right, one_hot(jnp.concatenate([targets, negatives], axis=1), rows))
+    for first in range(0, width, span):
+        part = slice(first, first + span)
+        tails = picked[:, part]
+        cands = picked[:, width + first : width + first + span].astype(bf16)
+        span_gradients(tails, cands, heads[:, part], rel[:, part], query[:, part], [o.at[:, part] for o in outs])
+
+
+def span_gradients(tails, cands, heads, rel, query, outs):
+    heads_out, tails_out, cands_out, rels_out = outs
     query32 = query.astype(f32)
     positive = jnp.sum(query32 * tails, axis=0, keepdims=True)
     scores = dot_nn(cands.T, query)
@@ -120,7 +131,7 @@
     query_ref[...] = query
 
 
-def gradient_kernel(ids_ref, heads_ref, rel_ref, query_ref, partner_ref, *rest):
+def gradient_kernel(span, ids_ref, heads_ref, rel_ref, query_ref, partner_ref, *rest):
     *outs, right = rest
 
     @pl.when(pl.program_id(0) == 0)
@@ -129,11 +140,11 @@
 
     ids = ids_ref[...]
     heads = heads_ref[...].astype(f32)
-    make_gradients(ids[2:3], ids[3:4], heads, rel_ref[...], query_ref[...], right[...], *outs)
-
-
-def paired_kernel(home_ref, ids_ref, own_ref, met_ref, passed_ref, table_ref, *rest):
-    *outs, left, right = rest
+    make_gradients(span, ids[2:3], ids[3:4], heads, rel_ref[...], query_ref[...], right[...], outs)
+
+
+def paired_kernel(span, home_ref, ids_ref, sent_ref, own_ref, met_ref, passed_ref, table_ref, *rest):
+    *outs, ids_out, left, right = rest
 
     @pl.when(pl.program_id(0) == 0)
     def _():
@@ -147,9 +158,10 @@
         def _():
             left[...] = passed_ref[...].T
 
-    ids = ids_ref[...]
+    ids = jnp.where(home_ref[0] == 1, ids_ref[...], sent_ref[...])
+    ids_out[...] = ids
     heads, rel, query = make_query(ids[0:1], ids[1:2], left[...], table_ref[...])
-    make_gradients(ids[2:3], ids[3:4], heads, rel, query, right[...], *outs)
+    make_gradients(span, ids[2:3], ids[3:4], heads, rel, query, right[...], outs)
 
 
 def gradient_shapes(features, edges):
@@ -164,14 +176,14 @@
     return pl.CostEstimate(flops=1 << 40, bytes_accessed=1 << 32, transcendentals=0)
 
 
-def query_call(ids, own, relation, rel_rows, span):
+def query_call(ids, own, relation, rel_rows, width):
     edges = ids.shape[1]
     rows, features = own.shape
     return pl.pallas_call(
         query_kernel,
-        grid=(edges // span,),
-        in_specs=[across(4, span), whole(own.shape), whole(relation.shape)],
-        out_specs=[across(features, span)] * 3 + [whole((2 * features, rel_rows))],
+        grid=(edges // width,),
+        in_specs=[across(4, width), whole(own.shape), whole(relation.shape)],
+        out_specs=[across(features, width)] * 3 + [whole((2 * features, rel_rows))],
         out_shape=[
             jax.ShapeDtypeStruct((features, edges), bf16),
             jax.ShapeDtypeStruct((features, edges), f32),
@@ -185,14 +197,14 @@
     )(ids, own, relation)
 
 
-def gradient_call(ids, heads, rel, query, partner, span):
+def gradient_call(ids, heads, rel, query, partner, span, width):
     features, edges = heads.shape
     rows = partner.shape[0]
     return pl.pallas_call(
-        gradient_kernel,
-        grid=(edges // span,),
-        in_specs=[across(4, span)] + [across(features, span)] * 3 + [whole(partner.shape)],
-        out_specs=gradient_specs(features, span),
+        functools.partial(gradient_kernel, span),
+        grid=(edges // width,),
+        in_specs=[across(4, width)] + [across(features, width)] * 3 + [whole(partner.shape)],
+        out_specs=gradient_specs(features, width),
         out_shape=gradient_shapes(features, edges),
         scratch_shapes=[pltpu.VMEM((features, rows), bf16)],
         compiler_params=params(),
@@ -201,22 +213,22 @@
     )(ids, heads, rel, query, partner)
 
 
-def paired_call(home, ids, own, met, passed, table, span):
+def paired_call(home, ids, sent_ids, own, met, passed, table, span, width):
     edges = ids.shape[1]
     rows, features = own.shape
     return pl.pallas_call(
-        paired_kernel,
-        grid=(edges // span,),
-        in_specs=[pl.BlockSpec(memory_space=pltpu.SMEM), across(4, span)]
+        functools.partial(paired_kernel, span),
+        grid=(edges // width,),
+        in_specs=[pl.BlockSpec(memory_space=pltpu.SMEM), across(4, width), across(4, width)]
         + [whole(own.shape)] * 3
         + [whole(table.shape)],
-        out_specs=gradient_specs(features, span),
-        out_shape=gradient_shapes(features, edges),
+        out_specs=gradient_specs(features, width) + [across(4, width)],
+        out_shape=gradient_shapes(features, edges) + [jax.ShapeDtypeStruct(ids.shape, jnp.int32)],
         scratch_shapes=[pltpu.VMEM((features, rows), bf16)] * 2,
         compiler_params=params(),
         cost_estimate=cost(5, edges, features, rows),
         name="paired",
-    )(home, ids, own, met, passed, table)
+    )(home, ids, sent_ids, own, met, passed, table)
 
 
 def scatter_kernel(chunk, lines, n_starts, *refs):
@@ -261,20 +273,21 @@
     return outs[0] if len(outs) == 1 else outs
 
 
-def adagrad_lines(grad, acc):
-    rows = grad.shape[0]
+def adagrad(grad, acc):
+    rows, features = grad.shape
     mean = jnp.mean(grad * grad, axis=1, keepdims=True)
-    acc_new = acc + jnp.broadcast_to(mean, (rows, 128)).T[:1]
+    acc_new = jnp.broadcast_to(acc, (128, rows)).T + mean
     scale = learn_rate / jnp.sqrt(acc_new)
-    return acc_new, jnp.broadcast_to(scale, (128, rows)).T[:, :1]
+    steps = [grad[:, k : k + 128] * scale for k in range(0, features, 128)]
+    return acc_new.T[:1], jnp.concatenate(steps, axis=1)
 
 
 def update_kernel(home_ref, entity_ref, acc_ref, local_ref, outer_ref, inner_ref, back_ref, new_ref, acc_new_ref):
     grad = local_ref[...] + outer_ref[...].astype(f32) + back_ref[...].astype(f32)
     grad = grad + jnp.where(home_ref[0] == 1, inner_ref[...].astype(f32), 0.0)
-    acc_new, scale = adagrad_lines(grad, acc_ref[...])
+    acc_new, step = adagrad(grad, acc_ref[...])
     acc_new_ref[...] = acc_new
-    new_ref[...] = (entity_ref[...].astype(f32) - scale * grad).astype(bf16)
+    new_ref[...] = (entity_ref[...].astype(f32) - step).astype(bf16)
 
 
 def update_call(home, entity, acc, local, outer, inner, back, chunk=512):
@@ -297,9 +310,9 @@
 def relation_kernel(relation_ref, acc_ref, total_ref, new_ref, acc_new_ref):
     n_rel = relation_ref.shape[0]
     total = total_ref[...].astype(f32)
-    acc_new, scale = adagrad_lines(total, acc_ref[...])
+    acc_new, step = adagrad(total, acc_ref[...])
     acc_new_ref[...] = acc_new[:, :n_rel]
-    new_ref[...] = relation_ref[...] - scale[:n_rel] * total[:n_rel]
+    new_ref[...] = relation_ref[...] - step[:n_rel]
 
 
 def relation_call(relation, acc, total):
@@ -342,6 +355,7 @@
     n_rel = relation.shape[0]
     spans, span = negatives.shape[2:]
     edges = spans * span
+    width = span * (2 - spans % 2)
     step = max(128, 8 * groups * doms)
     rel_rows = -(-n_rel // step) * step
 
@@ -375,15 +389,16 @@
     ids_one, ids_two = lines_call(edge_src, edge_rel, edge_dst, negatives.transpose(0, 2, 1, 3))
     met = send(entity, meeting)
     outer = send(entity, lambda g, d: (g + 1, d))
-    heads, rel, query, table = query_call(ids_two, entity, relation, rel_rows, span)
-    dl_two, dt_two, dc_two, dp_two = gradient_call(ids_two, heads, rel, query, outer, span)
+    heads, rel, query, table = query_call(ids_two, entity, relation, rel_rows, width)
+    dl_two, dt_two, dc_two, dp_two = gradient_call(ids_two, heads, rel, query, outer, span, width)
     met, ids_one, dt_two = lax.optimization_barrier((met, ids_one, dt_two))
     passed = send(met, neighbour, is_home)
     sent_ids = send(ids_one, lambda g, d: (g ^ 1, d + half), guest)
     rel_part = scatter_call([(ids_two, 1, dp_two)], rel_rows, [f32])
     passed, sent_ids, rel_part = lax.optimization_barrier((passed, sent_ids, rel_part))
-    ids_one = jnp.where(home == 1, ids_one, sent_ids)
-    dl_one, dt_one, dc_one, dp_one = paired_call(home, ids_one, entity, met, passed, table, span)
+    dl_one, dt_one, dc_one, dp_one, ids_one = paired_call(
+        home, ids_one, sent_ids, entity, met, passed, table, span, width
+    )
 
     left_one = scatter_call([(ids_one, 0, dl_one)], rows, [bf16])
     guest_left = send(left_one, neighbour, guest)

time: 145 us -> 141 us (0.972)
  Pallas kernels: 104 us -> 101 us
    pallas_call x3, Pallas kernels: 52.7 us -> 49.9 us  [the longest x1 23.1 us: paired_call(): pl.pallas_call(functools.partial(paired_kernel, span), grid=(edges // wid...]
  transfers between devices with their start and end apart: 10 -> 10, of which waited for: 3 -> 3; matrix products, arithmetic and copies ran while one was open for 0% -> 0% of each run, Pallas kernels for 42% -> 43%
where the time goes in v3:
time: 141 us; the launch traced here: 140 us
  Pallas kernels  101 us (72%)
  starting transfers between devices  25.7 us (18%)
  waiting for transfers between devices  10.9 us (8%)
  local copies, waits for them, and re-layouts  1.81 us (1%)
    pallas_call x6, Pallas kernels, scatter_call(): pl.pallas_call(kernel, grid=(rows // chunk,), in_specs=specs, out_specs=[...  38.1 us
    pallas_call x1, Pallas kernels, paired_call(): pl.pallas_call(functools.partial(paired_kernel, span), grid=(edges // wid...  23.1 us
    pallas_call x1, Pallas kernels, gradient_call(): pl.pallas_call(functools.partial(gradient_kernel, span), grid=(edges // w...  16.5 us
    ppermute x7, starting transfers between devices, send(): return lax.ppermute(block, axes, route)  13.4 us
    all_to_all x3, starting transfers between devices, exchange(): lax.all_to_all(pieces, axes, 0, 0, axis_index_groups=sets, tiled=True)  12.3 us
    pallas_call x1, Pallas kernels, query_call(): pl.pallas_call(query_kernel, grid=(edges // width,), in_specs=[across(4,...  10.3 us
    all_to_all x3, waiting for transfers between devices, exchange(): lax.all_to_all(pieces, axes, 0, 0, axis_index_groups=sets, tiled=True)  7.62 us
    pallas_call x1, Pallas kernels, update_call(): pl.pallas_call(update_kernel, grid=(rows // chunk,), in_specs=[pl.BlockSp...  4.94 us
  transfers between devices with their start and end apart: 10, of which 3 were waited for; matrix products, arithmetic and copies ran while one was open for 0% of the time, Pallas kernels for 43%

profile of v3, /device:TPU:0, one launch (start us, length us, event | category | flops | bytes accessed | tf_op | source)
XLA Modules:
  0.0 140.0 jit_solution(4058620162807852947)
XLA Ops:
  0.6 0.5 collective-permute-start.1
  1.1 2.6 %collective-permute-start = (bf16[2048,256]{1,0:T(8,128)(2,1)}, bf16[2048,256]{1,0:T(8,128)(2,1)}, u32[]{:S(2)}, u32[]{:S(2)}) collective-permute-start(bf16[2048,256]{1,0:T(8,128)(2,1)} %entity_ref.1), channel_id=1, source_target_pairs={{0,8},{1,9},{2,10},{3,11},{4,0},{5,1},{6,2},{7,3},{8,12},{9,13},{1... | collective-permute-start | bytes 3145736 | tf_op jit(solution)/shard_map/ppermute | solution.py:373
  3.8 0.0 copy-start.3
  3.8 1.5 %lines.1 = (s32[4,3072]{1,0:T(4,128)}, s32[4,3072]{1,0:T(4,128)}) custom-call(s32[1,2,3072]{2,1,0:T(2,128)} %source_ref.1, s32[1,2,3072]{2,1,0:T(2,128)} %rel_ref.1, s32[1,2,3072]{2,1,0:T(2,128)} %target_ref.1, s32[1,6,2,512]{3,2,1,0:T(2,128)} %bitcast.10), custom_call_target="tpu_custom_call" | custom-call | flops 1099511627776 | bytes 4294967296 | tf_op jit(solution)/shard_map/lines/pallas_call | solution.py:105
  5.3 0.0 copy-done.3
  5.3 0.0 copy-start.7
  5.3 0.8 copy-done.7
  6.1 0.0 copy-start.8
  6.1 10.3 %queries.1 = (bf16[256,3072]{1,0:T(8,128)(2,1)}, f32[256,3072]{1,0:T(8,128)}, bf16[256,3072]{1,0:T(8,128)(2,1)}, bf16[512,1024]{1,0:T(8,128)(2,1)}) custom-call(s32[4,3072]{1,0:T(4,128)S(1)} %copy-done.7, bf16[2048,256]{1,0:T(8,128)(2,1)} %entity_ref.1, f32[1000,256]{1,0:T(8,128)S(1)} %copy-done.3), custom_call_target="tpu_custom_call" | custom-call | flops 1099511627776 | bytes 4294967296 | tf_op jit(solution)/shard_map/queries/pallas_call | solution.py:182
  16.4 0.0 collective-permute-done.1.partner_ref
  16.4 0.0 copy-done.8
  16.4 16.5 %gradients.1 = (bf16[256,3072]{1,0:T(8,128)(2,1)}, bf16[256,3072]{1,0:T(8,128)(2,1)}, bf16[256,3072]{1,0:T(8,128)(2,1)}, bf16[256,3072]{1,0:T(8,128)(2,1)}) custom-call(s32[4,3072]{1,0:T(4,128)S(1)} %copy-done.8, bf16[256,3072]{1,0:T(8,128)(2,1)} %get-tuple-element.38.heads_ref, f32[256,3072]{1,0:T(8,128)} %get-tuple-element.39.rel_ref, ...), custom_call_target="tpu_custom_call" | custom-call | flops 1099511627776 | bytes 4294967296 | tf_op jit(solution)/shard_map/gradients/pallas_call | solution.py:203
  32.9 0.0 collective-permute-done.met_ref
  32.9 5.2 %collective-permute-start.2 = (bf16[2048,256]{1,0:T(8,128)(2,1)}, bf16[2048,256]{1,0:T(8,128)(2,1)}, u32[]{:S(2)}, u32[]{:S(2)}) collective-permute-start(bf16[2048,256]{1,0:T(8,128)(2,1)} %collective-permute-done.met_ref), channel_id=1, source_target_pairs={{0,8},{1,9},{2,10},{3,11},{12,4},{13,5},{14,6},{15,7},{16,24},{17,... | collective-permute-start | bytes 3145736 | tf_op jit(solution)/shard_map/ppermute | solution.py:373
  38.1 1.3 collective-permute-start.3
  39.4 0.0 copy-start
  39.4 3.5 %scatter.6.refs_2_ = f32[1024,256]{1,0:T(8,128)S(1)} custom-call(s32[4,3072]{1,0:T(4,128)S(1)} %copy-done.8, bf16[256,3072]{1,0:T(8,128)(2,1)} %get-tuple-element.44.refs_1_), custom_call_target="tpu_custom_call" | custom-call | flops 1099511627776 | bytes 4294967296 | tf_op jit(solution)/shard_map/scatter/pallas_call | solution.py:263
  42.9 0.0 collective-permute-done.3.sent_ref
  42.9 0.0 collective-permute-done.2.passed_ref
  42.9 0.0 copy-done
  43.0 23.1 %paired.1 = (bf16[256,3072]{1,0:T(8,128)(2,1)}, bf16[256,3072]{1,0:T(8,128)(2,1)}, bf16[256,3072]{1,0:T(8,128)(2,1)}, bf16[256,3072]{1,0:T(8,128)(2,1)}, s32[4,3072]{1,0:T(4,128)S(1)}) custom-call(s32[1]{0:T(128)} %bitcast.home_ref, s32[4,3072]{1,0:T(4,128)} %get-tuple-element.42.ids_ref, s32[4,3072]{1,0:T(4,128)} %collective-permute-done.3.sent_ref, ...), custom_call_target="tpu_custom_call" | custom-call | flops 1099511627776 | bytes 4294967296 | tf_op jit(solution)/shard_map/paired/pallas_call | solution.py:219
  66.1 0.0 copy-start.10
  66.1 5.5 %scatter.7.inner_ref = bf16[2048,256]{1,0:T(8,128)(2,1)S(1)} custom-call(s32[4,3072]{1,0:T(4,128)S(1)} %get-tuple-element.48.refs_0_.refs_2_, bf16[256,3072]{1,0:T(8,128)(2,1)} %get-tuple-element.51.refs_1_), custom_call_target="tpu_custom_call" | custom-call | flops 1099511627776 | bytes 4294967296 | tf_op jit(solution)/shard_map/scatter/pallas_call | solution.py:263
  71.6 0.0 copy-start.2
  71.6 1.3 collective-permute-start.4
  72.9 0.0 copy-done.2
  72.9 0.0 copy-done.10
  72.9 3.2 %collective-permute-done.4.refs_4_ = bf16[2048,256]{1,0:T(8,128)(2,1)S(1)} collective-permute-done((bf16[2048,256]{1,0:T(8,128)(2,1)S(1)}, bf16[2048,256]{1,0:T(8,128)(2,1)S(1)}, u32[]{:S(2)}, u32[]{:S(2)}) %collective-permute-start.4) | collective-permute-done | bytes 1048608 | tf_op jit(solution)/shard_map/ppermute | solution.py:373
  76.1 0.0 copy-start.11
  76.1 1.0 copy-done.11
  77.1 10.0 %scatter.8 = bf16[2048,256]{1,0:T(8,128)(2,1)} custom-call(s32[4,3072]{1,0:T(4,128)S(1)} %get-tuple-element.48.refs_0_.refs_2_, bf16[256,3072]{1,0:T(8,128)(2,1)} %get-tuple-element.49.refs_1_, s32[4,3072]{1,0:T(4,128)S(1)} %get-tuple-element.48.refs_0_.refs_2_, bf16[256,3072]{1,0:T(8,128)(2,1)} %get-tuple-element.50.refs_3_, bf16[2048,256]{1,0:T(8,128)(2,1)} %copy-done.11), custom_call_target="tpu_custom_call" | custom-call | flops 1099511627776 | bytes 4294967296 | tf_op jit(solution)/shard_map/scatter/pallas_call | solution.py:263
  87.2 0.8 collective-permute-start.6
  88.0 4.2 %scatter.9 = bf16[1024,256]{1,0:T(8,128)(2,1)} custom-call(s32[4,3072]{1,0:T(4,128)S(1)} %get-tuple-element.48.refs_0_.refs_2_, bf16[256,3072]{1,0:T(8,128)(2,1)} %get-tuple-element.55.refs_1_, f32[1024,256]{1,0:T(8,128)S(1)} %scatter.6.refs_2_), custom_call_target="tpu_custom_call" | custom-call | flops 1099511627776 | bytes 4294967296 | tf_op jit(solution)/shard_map/scatter/pallas_call | solution.py:263
  92.2 4.1 %all-to-all-start = ((bf16[8,128,256]{2,1,0:T(8,128)(2,1)}), bf16[8,128,256]{2,1,0:T(8,128)(2,1)}, u32[]{:S(2)}, u32[]{:S(2)}) async-start(bf16[8,128,256]{2,1,0:T(8,128)(2,1)} %bitcast.3), calls=%async_computation | async-start | bytes 1048576 | tf_op jit(solution)/shard_map/all_to_all | solution.py:413
  96.3 9.9 %scatter.10 = bf16[2048,256]{1,0:T(8,128)(2,1)} custom-call(s32[4,3072]{1,0:T(4,128)S(1)} %copy-done.8, bf16[256,3072]{1,0:T(8,128)(2,1)} %get-tuple-element.58.refs_1_, s32[4,3072]{1,0:T(4,128)S(1)} %copy-done.8, bf16[256,3072]{1,0:T(8,128)(2,1)} %get-tuple-element.59.refs_3_), custom_call_target="tpu_custom_call" | custom-call | flops 1099511627776 | bytes 4294967296 | tf_op jit(solution)/shard_map/scatter/pallas_call | solution.py:263
  106.2 1.6 %collective-permute-start.5 = (bf16[2048,256]{1,0:T(8,128)(2,1)}, bf16[2048,256]{1,0:T(8,128)(2,1)}, u32[]{:S(2)}, u32[]{:S(2)}) collective-permute-start(bf16[2048,256]{1,0:T(8,128)(2,1)} %scatter.10), channel_id=1, source_target_pairs={{0,24},{1,25},{2,26},{3,27},{4,28},{5,29},{6,30},{7,31},{8,0},{9,1... | collective-permute-start | bytes 3145736 | tf_op jit(solution)/shard_map/ppermute | solution.py:373
  107.9 0.0 all-to-all-done.pieces_ref
  107.9 0.0 copy-start.6
  107.9 0.0 copy-start.9
  107.9 1.9 %shares.2 = bf16[4,128,256]{2,1,0:T(8,128)(2,1)} custom-call(bf16[8,128,256]{2,1,0:T(8,128)(2,1)} %all-to-all-done.pieces_ref), custom_call_target="tpu_custom_call" | custom-call | flops 1099511627776 | bytes 4294967296 | tf_op jit(solution)/shard_map/shares/pallas_call | solution.py:340
  109.8 4.0 %all-to-all-start.1 = ((bf16[4,128,256]{2,1,0:T(8,128)(2,1)}), bf16[4,128,256]{2,1,0:T(8,128)(2,1)}, u32[]{:S(2)}, u32[]{:S(2)}) async-start(bf16[4,128,256]{2,1,0:T(8,128)(2,1)} %shares.2), calls=%async_computation.1 | async-start | bytes 524288 | tf_op jit(solution)/shard_map/all_to_all | solution.py:413
  113.9 0.0 copy-done.6
  113.9 0.0 copy-done.9
  113.9 4.9 %scatter.11.local_ref = f32[2048,256]{1,0:T(8,128)} custom-call(s32[4,3072]{1,0:T(4,128)S(1)} %copy-done.9, bf16[256,3072]{1,0:T(8,128)(2,1)S(1)} %copy-done.6), custom_call_target="tpu_custom_call" | custom-call | flops 1099511627776 | bytes 4294967296 | tf_op jit(solution)/shard_map/scatter/pallas_call | solution.py:263
  118.8 3.3 %all-to-all-done.1.pieces_ref = bf16[4,128,256]{2,1,0:T(8,128)(2,1)} async-done(((bf16[4,128,256]{2,1,0:T(8,128)(2,1)}), bf16[4,128,256]{2,1,0:T(8,128)(2,1)}, u32[]{:S(2)}, u32[]{:S(2)}) %all-to-all-start.1) | async-done | bytes 262176 | tf_op jit(solution)/shard_map/all_to_all | solution.py:413
  122.1 0.0 copy-start.1
  122.1 0.0 copy-start.5
  122.1 1.9 %shares.3 = bf16[8,128,256]{2,1,0:T(8,128)(2,1)} custom-call(bf16[4,128,256]{2,1,0:T(8,128)(2,1)} %all-to-all-done.1.pieces_ref), custom_call_target="tpu_custom_call" | custom-call | flops 1099511627776 | bytes 4294967296 | tf_op jit(solution)/shard_map/shares/pallas_call | solution.py:340
  124.0 4.2 %all-to-all-start.2 = ((bf16[8,128,256]{2,1,0:T(8,128)(2,1)}), bf16[8,128,256]{2,1,0:T(8,128)(2,1)}, u32[]{:S(2)}, u32[]{:S(2)}) async-start(bf16[8,128,256]{2,1,0:T(8,128)(2,1)} %shares.3), calls=%async_computation.2 | async-start | bytes 1048576 | tf_op jit(solution)/shard_map/all_to_all | solution.py:413
  128.2 0.0 collective-permute-done.5.outer_ref
  128.2 0.0 collective-permute-done.6.back_ref
  128.2 0.0 copy-done.1
  128.2 0.0 copy-done.5
  128.2 0.0 copy-start.4
  128.2 4.9 %update.1 = (bf16[2048,256]{1,0:T(8,128)(2,1)}, f32[1,2048]{1,0:T(1,128)}) custom-call(s32[1]{0:T(128)} %bitcast.home_ref, bf16[2048,256]{1,0:T(8,128)(2,1)S(1)} %copy-done.1, f32[1,2048]{1,0:T(1,128)S(1)} %bitcast.8, f32[2048,256]{1,0:T(8,128)} %scatter.11.local_ref, bf16[2048,256]{1,0:T(8,128)(2,1)} %collective-permute-done.5.outer_ref, ...), custom_call_target="tpu_custom_call" | custom-call | flops 1099511627776 | bytes 4294967296 | tf_op jit(solution)/shard_map/update/pallas_call | solution.py:297
  133.2 4.3 %all-to-all-done.2 = bf16[8,128,256]{2,1,0:T(8,128)(2,1)} async-done(((bf16[8,128,256]{2,1,0:T(8,128)(2,1)}), bf16[8,128,256]{2,1,0:T(8,128)(2,1)}, u32[]{:S(2)}, u32[]{:S(2)}) %all-to-all-start.2) | async-done | bytes 524320 | tf_op jit(solution)/shard_map/all_to_all | solution.py:413
  137.4 0.0 copy-done.4
  137.4 2.5 %relation.1 = (f32[1000,256]{1,0:T(8,128)}, f32[1,1000]{1,0:T(1,128)}) custom-call(f32[1000,256]{1,0:T(8,128)S(1)} %copy-done.4, f32[1,1024]{1,0:T(1,128)S(1)} %pad.4.acc_ref, bf16[1024,256]{1,0:T(8,128)(2,1)} %bitcast.6.total_ref), custom_call_target="tpu_custom_call" | custom-call | flops 1099511627776 | bytes 4294967296 | tf_op jit(solution)/shard_map/relation/pallas_call | solution.py:321
  (1 shorter events, 0.0 us)
Async XLA Ops:
  0.6 15.8 %collective-permute-start.1 = (bf16[2048,256]{1,0:T(8,128)(2,1)}, bf16[2048,256]{1,0:T(8,128)(2,1)}, u32[]{:S(2)}, u32[]{:S(2)}) collective-permute-start(bf16[2048,256]{1,0:T(8,128)(2,1)} %entity_ref.1), channel_id=1, source_target_pairs={{0,8},{1,9},{2,10},{3,11},{4,12},{5,13},{6,14},{7,15},{8,16},{9,17... | collective-permute-start | bytes 3145736 | tf_op jit(solution)/shard_map/ppermute | solution.py:373
  1.1 31.8 %collective-permute-start = (bf16[2048,256]{1,0:T(8,128)(2,1)}, bf16[2048,256]{1,0:T(8,128)(2,1)}, u32[]{:S(2)}, u32[]{:S(2)}) collective-permute-start(bf16[2048,256]{1,0:T(8,128)(2,1)} %entity_ref.1), channel_id=1, source_target_pairs={{0,8},{1,9},{2,10},{3,11},{4,0},{5,1},{6,2},{7,3},{8,12},{9,13},{1... | collective-permute-start | bytes 3145736 | tf_op jit(solution)/shard_map/ppermute | solution.py:373
  3.8 1.5 %copy-start.3 = (f32[1000,256]{1,0:T(8,128)S(1)}, f32[1000,256]{1,0:T(8,128)}, u32[]{:S(2)}) copy-start(f32[1000,256]{1,0:T(8,128)} %relation_ref.3) | copy-start | bytes 3072004
  5.3 0.8 copy-start.7
  6.1 10.3 %copy-start.8 = (s32[4,3072]{1,0:T(4,128)S(1)}, s32[4,3072]{1,0:T(4,128)}, u32[]{:S(2)}) copy-start(s32[4,3072]{1,0:T(4,128)} %get-tuple-element.37.ids_ref.refs_0_.refs_2_) | copy-start | bytes 147460
  32.9 10.0 %collective-permute-start.2 = (bf16[2048,256]{1,0:T(8,128)(2,1)}, bf16[2048,256]{1,0:T(8,128)(2,1)}, u32[]{:S(2)}, u32[]{:S(2)}) collective-permute-start(bf16[2048,256]{1,0:T(8,128)(2,1)} %collective-permute-done.met_ref), channel_id=1, source_target_pairs={{0,8},{1,9},{2,10},{3,11},{12,4},{13,5},{14,6},{15,7},{16,24},{17,... | collective-permute-start | bytes 3145736 | tf_op jit(solution)/shard_map/ppermute | solution.py:373
  38.1 4.8 %collective-permute-start.3 = (s32[4,3072]{1,0:T(4,128)}, s32[4,3072]{1,0:T(4,128)}, u32[]{:S(2)}, u32[]{:S(2)}) collective-permute-start(s32[4,3072]{1,0:T(4,128)} %get-tuple-element.42.ids_ref), channel_id=1, source_target_pairs={{4,8},{5,9},{6,10},{7,11},{8,4},{9,5},{10,6},{11,7},{20,24},{21,25... | collective-permute-start | bytes 147464 | tf_op jit(solution)/shard_map/ppermute | solution.py:373
  39.4 3.6 %copy-start = (bf16[2048,256]{1,0:T(8,128)(2,1)S(1)}, bf16[2048,256]{1,0:T(8,128)(2,1)}, u32[]{:S(2)}) copy-start(bf16[2048,256]{1,0:T(8,128)(2,1)} %entity_ref.1) | copy-start | bytes 3145732
  66.1 6.8 %copy-start.10 = (f32[1000]{0:T(1024)S(1)}, f32[1000]{0:T(1024)}, u32[]{:S(2)}) copy-start(f32[1000]{0:T(1024)} %param.11) | copy-start | bytes 12004
  71.6 1.3 copy-start.2
  71.6 4.6 %collective-permute-start.4 = (bf16[2048,256]{1,0:T(8,128)(2,1)S(1)}, bf16[2048,256]{1,0:T(8,128)(2,1)S(1)}, u32[]{:S(2)}, u32[]{:S(2)}) collective-permute-start(bf16[2048,256]{1,0:T(8,128)(2,1)S(1)} %scatter.7.inner_ref), channel_id=1, source_target_pairs={{4,12},{5,13},{6,14},{7,15},{8,0},{9,1},{10,2},{11,3},{20,28},{21,... | collective-permute-start | bytes 3145736 | tf_op jit(solution)/shard_map/ppermute | solution.py:373
  76.1 1.0 copy-start.11
  87.2 41.0 %collective-permute-start.6 = (bf16[2048,256]{1,0:T(8,128)(2,1)}, bf16[2048,256]{1,0:T(8,128)(2,1)}, u32[]{:S(2)}, u32[]{:S(2)}) collective-permute-start(bf16[2048,256]{1,0:T(8,128)(2,1)} %scatter.8), channel_id=1, source_target_pairs={{0,4},{1,5},{2,6},{3,7},{4,12},{5,13},{6,14},{7,15},{8,0},{9,1},{1... | collective-permute-start | bytes 3145736 | tf_op jit(solution)/shard_map/ppermute | solution.py:373
  92.2 15.7 %all-to-all-start = ((bf16[8,128,256]{2,1,0:T(8,128)(2,1)}), bf16[8,128,256]{2,1,0:T(8,128)(2,1)}, u32[]{:S(2)}, u32[]{:S(2)}) async-start(bf16[8,128,256]{2,1,0:T(8,128)(2,1)} %bitcast.3), calls=%async_computation | async-start | bytes 1048576 | tf_op jit(solution)/shard_map/all_to_all | solution.py:413
  106.2 21.9 %collective-permute-start.5 = (bf16[2048,256]{1,0:T(8,128)(2,1)}, bf16[2048,256]{1,0:T(8,128)(2,1)}, u32[]{:S(2)}, u32[]{:S(2)}) collective-permute-start(bf16[2048,256]{1,0:T(8,128)(2,1)} %scatter.10), channel_id=1, source_target_pairs={{0,24},{1,25},{2,26},{3,27},{4,28},{5,29},{6,30},{7,31},{8,0},{9,1... | collective-permute-start | bytes 3145736 | tf_op jit(solution)/shard_map/ppermute | solution.py:373
  107.9 6.0 %copy-start.6 = (bf16[256,3072]{1,0:T(8,128)(2,1)S(1)}, bf16[256,3072]{1,0:T(8,128)(2,1)}, u32[]{:S(2)}) copy-start(bf16[256,3072]{1,0:T(8,128)(2,1)} %get-tuple-element.61.refs_1_) | copy-start | bytes 4718596
  107.9 6.0 %copy-start.9 = (s32[4,3072]{1,0:T(4,128)S(1)}, s32[4,3072]{1,0:T(4,128)}, u32[]{:S(2)}) copy-start(s32[4,3072]{1,0:T(4,128)} %get-tuple-element.37.ids_ref.refs_0_.refs_2_) | copy-start | bytes 147460
  109.8 12.3 %all-to-all-start.1 = ((bf16[4,128,256]{2,1,0:T(8,128)(2,1)}), bf16[4,128,256]{2,1,0:T(8,128)(2,1)}, u32[]{:S(2)}, u32[]{:S(2)}) async-start(bf16[4,128,256]{2,1,0:T(8,128)(2,1)} %shares.2), calls=%async_computation.1 | async-start | bytes 524288 | tf_op jit(solution)/shard_map/all_to_all | solution.py:413
  122.1 6.1 %copy-start.1 = (bf16[2048,256]{1,0:T(8,128)(2,1)S(1)}, bf16[2048,256]{1,0:T(8,128)(2,1)}, u32[]{:S(2)}) copy-start(bf16[2048,256]{1,0:T(8,128)(2,1)} %entity_ref.1) | copy-start | bytes 3145732
  122.1 6.1 %copy-start.5 = (f32[2048]{0:T(1024)S(1)}, f32[2048]{0:T(1024)}, u32[]{:S(2)}) copy-start(f32[2048]{0:T(1024)} %param.9) | copy-start | bytes 24580
  124.0 13.4 %all-to-all-start.2 = ((bf16[8,128,256]{2,1,0:T(8,128)(2,1)}), bf16[8,128,256]{2,1,0:T(8,128)(2,1)}, u32[]{:S(2)}, u32[]{:S(2)}) async-start(bf16[8,128,256]{2,1,0:T(8,128)(2,1)} %shares.3), calls=%async_computation.2 | async-start | bytes 1048576 | tf_op jit(solution)/shard_map/all_to_all | solution.py:413
  128.2 9.2 %copy-start.4 = (f32[1000,256]{1,0:T(8,128)S(1)}, f32[1000,256]{1,0:T(8,128)}, u32[]{:S(2)}) copy-start(f32[1000,256]{1,0:T(8,128)} %relation_ref.3) | copy-start | bytes 3072004

commit v4 on v3

--- a/solution.py
+++ b/solution.py
@@ -245,7 +245,7 @@
         out_ref[...] = total.astype(out_ref.dtype)
 
 
-def scatter_call(pairs, rows, dtypes, starts=(), chunk=512):
+def scatter_call(pairs, rows, dtypes, starts=(), chunk=1024):
     features = pairs[0][2].shape[0]
     chunk = min(chunk, rows)
     operands, specs = [], []
@@ -290,7 +290,7 @@
     new_ref[...] = (entity_ref[...].astype(f32) - step).astype(bf16)
 
 
-def update_call(home, entity, acc, local, outer, inner, back, chunk=512):
+def update_call(home, entity, acc, local, outer, inner, back, chunk=1024):
     rows, features = entity.shape
     down = pl.BlockSpec((chunk, features), lambda s: (s, 0))
     line = pl.BlockSpec((1, chunk), lambda s: (0, s))

time: 141 us -> 139 us (0.986)
  Pallas kernels: 101 us -> 98.3 us
    pallas_call x6, Pallas kernels: 38.1 us -> 36.4 us  [scatter_call(): pl.pallas_call(kernel, grid=(rows // chunk,), in_specs=specs, out_specs=[...]
  transfers between devices with their start and end apart: 10 -> 10, of which waited for: 3 -> 3; matrix products, arithmetic and copies ran while one was open for 0% -> 0% of each run, Pallas kernels for 43% -> 42%
where the time goes in v4:
time: 139 us
  Pallas kernels  98.3 us (71%)
  starting transfers between devices  25.7 us (18%)
  waiting for transfers between devices  12.2 us (9%)
  local copies, waits for them, and re-layouts  1.81 us (1%)
    pallas_call x6, Pallas kernels, scatter_call(): pl.pallas_call(kernel, grid=(rows // chunk,), in_specs=specs, out_specs=[...  36.4 us
    pallas_call x1, Pallas kernels, paired_call(): pl.pallas_call(functools.partial(paired_kernel, span), grid=(edges // wid...  23.1 us
    pallas_call x1, Pallas kernels, gradient_call(): pl.pallas_call(functools.partial(gradient_kernel, span), grid=(edges // w...  16.5 us
    ppermute x7, starting transfers between devices, send(): return lax.ppermute(block, axes, route)  13.1 us
    all_to_all x3, starting transfers between devices, exchange(): lax.all_to_all(pieces, axes, 0, 0, axis_index_groups=sets, tiled=True)  12.6 us
    pallas_call x1, Pallas kernels, query_call(): pl.pallas_call(query_kernel, grid=(edges // width,), in_specs=[across(4,...  10.3 us
    all_to_all x3, waiting for transfers between devices, exchange(): lax.all_to_all(pieces, axes, 0, 0, axis_index_groups=sets, tiled=True)  8.94 us
    pallas_call x1, Pallas kernels, update_call(): pl.pallas_call(update_kernel, grid=(rows // chunk,), in_specs=[pl.BlockSp...  4.07 us
  transfers between devices with their start and end apart: 10, of which 3 were waited for; matrix products, arithmetic and copies ran while one was open for 0% of the time, Pallas kernels for 42%

profile of v4, /device:TPU:0, one launch (start us, length us, event | category | flops | bytes accessed | tf_op | source)
XLA Modules:
  0.0 138.7 jit_solution(8006531027819300919)
XLA Ops:
  0.6 0.5 collective-permute-start.1
  1.1 2.6 %collective-permute-start = (bf16[2048,256]{1,0:T(8,128)(2,1)}, bf16[2048,256]{1,0:T(8,128)(2,1)}, u32[]{:S(2)}, u32[]{:S(2)}) collective-permute-start(bf16[2048,256]{1,0:T(8,128)(2,1)} %entity_ref.1), channel_id=1, source_target_pairs={{0,8},{1,9},{2,10},{3,11},{4,0},{5,1},{6,2},{7,3},{8,12},{9,13},{1... | collective-permute-start | bytes 3145736 | tf_op jit(solution)/shard_map/ppermute | solution.py:373
  3.8 0.0 copy-start.3
  3.8 1.5 %lines.1 = (s32[4,3072]{1,0:T(4,128)}, s32[4,3072]{1,0:T(4,128)}) custom-call(s32[1,2,3072]{2,1,0:T(2,128)} %source_ref.1, s32[1,2,3072]{2,1,0:T(2,128)} %rel_ref.1, s32[1,2,3072]{2,1,0:T(2,128)} %target_ref.1, s32[1,6,2,512]{3,2,1,0:T(2,128)} %bitcast.10), custom_call_target="tpu_custom_call" | custom-call | flops 1099511627776 | bytes 4294967296 | tf_op jit(solution)/shard_map/lines/pallas_call | solution.py:105
  5.3 0.0 copy-done.3
  5.3 0.0 copy-start.7
  5.3 0.8 copy-done.7
  6.1 0.0 copy-start.8
  6.1 10.3 %queries.1 = (bf16[256,3072]{1,0:T(8,128)(2,1)}, f32[256,3072]{1,0:T(8,128)}, bf16[256,3072]{1,0:T(8,128)(2,1)}, bf16[512,1024]{1,0:T(8,128)(2,1)}) custom-call(s32[4,3072]{1,0:T(4,128)S(1)} %copy-done.7, bf16[2048,256]{1,0:T(8,128)(2,1)} %entity_ref.1, f32[1000,256]{1,0:T(8,128)S(1)} %copy-done.3), custom_call_target="tpu_custom_call" | custom-call | flops 1099511627776 | bytes 4294967296 | tf_op jit(solution)/shard_map/queries/pallas_call | solution.py:182
  16.4 0.0 collective-permute-done.1.partner_ref
  16.4 0.0 copy-done.8
  16.4 16.5 %gradients.1 = (bf16[256,3072]{1,0:T(8,128)(2,1)}, bf16[256,3072]{1,0:T(8,128)(2,1)}, bf16[256,3072]{1,0:T(8,128)(2,1)}, bf16[256,3072]{1,0:T(8,128)(2,1)}) custom-call(s32[4,3072]{1,0:T(4,128)S(1)} %copy-done.8, bf16[256,3072]{1,0:T(8,128)(2,1)} %get-tuple-element.38.heads_ref, f32[256,3072]{1,0:T(8,128)} %get-tuple-element.39.rel_ref, ...), custom_call_target="tpu_custom_call" | custom-call | flops 1099511627776 | bytes 4294967296 | tf_op jit(solution)/shard_map/gradients/pallas_call | solution.py:203
  32.9 0.0 collective-permute-done.met_ref
  32.9 5.2 %collective-permute-start.2 = (bf16[2048,256]{1,0:T(8,128)(2,1)}, bf16[2048,256]{1,0:T(8,128)(2,1)}, u32[]{:S(2)}, u32[]{:S(2)}) collective-permute-start(bf16[2048,256]{1,0:T(8,128)(2,1)} %collective-permute-done.met_ref), channel_id=1, source_target_pairs={{0,8},{1,9},{2,10},{3,11},{12,4},{13,5},{14,6},{15,7},{16,24},{17,... | collective-permute-start | bytes 3145736 | tf_op jit(solution)/shard_map/ppermute | solution.py:373
  38.1 1.3 collective-permute-start.3
  39.4 0.0 copy-start
  39.4 3.3 %scatter.6.refs_2_ = f32[1024,256]{1,0:T(8,128)S(1)} custom-call(s32[4,3072]{1,0:T(4,128)S(1)} %copy-done.8, bf16[256,3072]{1,0:T(8,128)(2,1)} %get-tuple-element.44.refs_1_), custom_call_target="tpu_custom_call" | custom-call | flops 1099511627776 | bytes 4294967296 | tf_op jit(solution)/shard_map/scatter/pallas_call | solution.py:263
  42.7 0.0 collective-permute-done.3.sent_ref
  42.7 0.0 collective-permute-done.2.passed_ref
  42.7 0.0 copy-done
  42.7 23.1 %paired.1 = (bf16[256,3072]{1,0:T(8,128)(2,1)}, bf16[256,3072]{1,0:T(8,128)(2,1)}, bf16[256,3072]{1,0:T(8,128)(2,1)}, bf16[256,3072]{1,0:T(8,128)(2,1)}, s32[4,3072]{1,0:T(4,128)S(1)}) custom-call(s32[1]{0:T(128)} %bitcast.home_ref, s32[4,3072]{1,0:T(4,128)} %get-tuple-element.42.ids_ref, s32[4,3072]{1,0:T(4,128)} %collective-permute-done.3.sent_ref, ...), custom_call_target="tpu_custom_call" | custom-call | flops 1099511627776 | bytes 4294967296 | tf_op jit(solution)/shard_map/paired/pallas_call | solution.py:219
  65.9 0.0 copy-start.10
  65.9 5.1 %scatter.7.inner_ref = bf16[2048,256]{1,0:T(8,128)(2,1)S(1)} custom-call(s32[4,3072]{1,0:T(4,128)S(1)} %get-tuple-element.48.refs_0_.refs_2_, bf16[256,3072]{1,0:T(8,128)(2,1)} %get-tuple-element.51.refs_1_), custom_call_target="tpu_custom_call" | custom-call | flops 1099511627776 | bytes 4294967296 | tf_op jit(solution)/shard_map/scatter/pallas_call | solution.py:263
  71.0 0.0 copy-start.2
  71.0 1.3 collective-permute-start.4
  72.3 0.0 copy-done.2
  72.3 0.0 copy-done.10
  72.3 3.2 %collective-permute-done.4.refs_4_ = bf16[2048,256]{1,0:T(8,128)(2,1)S(1)} collective-permute-done((bf16[2048,256]{1,0:T(8,128)(2,1)S(1)}, bf16[2048,256]{1,0:T(8,128)(2,1)S(1)}, u32[]{:S(2)}, u32[]{:S(2)}) %collective-permute-start.4) | collective-permute-done | bytes 1048608 | tf_op jit(solution)/shard_map/ppermute | solution.py:373
  75.5 0.0 copy-start.11
  75.5 1.0 copy-done.11
  76.5 9.8 %scatter.8 = bf16[2048,256]{1,0:T(8,128)(2,1)} custom-call(s32[4,3072]{1,0:T(4,128)S(1)} %get-tuple-element.48.refs_0_.refs_2_, bf16[256,3072]{1,0:T(8,128)(2,1)} %get-tuple-element.49.refs_1_, s32[4,3072]{1,0:T(4,128)S(1)} %get-tuple-element.48.refs_0_.refs_2_, bf16[256,3072]{1,0:T(8,128)(2,1)} %get-tuple-element.50.refs_3_, bf16[2048,256]{1,0:T(8,128)(2,1)} %copy-done.11), custom_call_target="tpu_custom_call" | custom-call | flops 1099511627776 | bytes 4294967296 | tf_op jit(solution)/shard_map/scatter/pallas_call | solution.py:263
  86.2 0.8 collective-permute-start.6
  87.0 4.0 %scatter.9 = bf16[1024,256]{1,0:T(8,128)(2,1)} custom-call(s32[4,3072]{1,0:T(4,128)S(1)} %get-tuple-element.48.refs_0_.refs_2_, bf16[256,3072]{1,0:T(8,128)(2,1)} %get-tuple-element.55.refs_1_, f32[1024,256]{1,0:T(8,128)S(1)} %scatter.6.refs_2_), custom_call_target="tpu_custom_call" | custom-call | flops 1099511627776 | bytes 4294967296 | tf_op jit(solution)/shard_map/scatter/pallas_call | solution.py:263
  91.1 4.4 %all-to-all-start = ((bf16[8,128,256]{2,1,0:T(8,128)(2,1)}), bf16[8,128,256]{2,1,0:T(8,128)(2,1)}, u32[]{:S(2)}, u32[]{:S(2)}) async-start(bf16[8,128,256]{2,1,0:T(8,128)(2,1)} %bitcast.3), calls=%async_computation | async-start | bytes 1048576 | tf_op jit(solution)/shard_map/all_to_all | solution.py:413
  95.4 9.6 %scatter.10 = bf16[2048,256]{1,0:T(8,128)(2,1)} custom-call(s32[4,3072]{1,0:T(4,128)S(1)} %copy-done.8, bf16[256,3072]{1,0:T(8,128)(2,1)} %get-tuple-element.58.refs_1_, s32[4,3072]{1,0:T(4,128)S(1)} %copy-done.8, bf16[256,3072]{1,0:T(8,128)(2,1)} %get-tuple-element.59.refs_3_), custom_call_target="tpu_custom_call" | custom-call | flops 1099511627776 | bytes 4294967296 | tf_op jit(solution)/shard_map/scatter/pallas_call | solution.py:263
  105.0 1.4 %collective-permute-start.5 = (bf16[2048,256]{1,0:T(8,128)(2,1)}, bf16[2048,256]{1,0:T(8,128)(2,1)}, u32[]{:S(2)}, u32[]{:S(2)}) collective-permute-start(bf16[2048,256]{1,0:T(8,128)(2,1)} %scatter.10), channel_id=1, source_target_pairs={{0,24},{1,25},{2,26},{3,27},{4,28},{5,29},{6,30},{7,31},{8,0},{9,1... | collective-permute-start | bytes 3145736 | tf_op jit(solution)/shard_map/ppermute | solution.py:373
  106.5 0.0 all-to-all-done.pieces_ref
  106.5 0.0 copy-start.6
  106.5 0.0 copy-start.9
  106.5 1.9 %shares.2 = bf16[4,128,256]{2,1,0:T(8,128)(2,1)} custom-call(bf16[8,128,256]{2,1,0:T(8,128)(2,1)} %all-to-all-done.pieces_ref), custom_call_target="tpu_custom_call" | custom-call | flops 1099511627776 | bytes 4294967296 | tf_op jit(solution)/shard_map/shares/pallas_call | solution.py:340
  108.4 4.0 %all-to-all-start.1 = ((bf16[4,128,256]{2,1,0:T(8,128)(2,1)}), bf16[4,128,256]{2,1,0:T(8,128)(2,1)}, u32[]{:S(2)}, u32[]{:S(2)}) async-start(bf16[4,128,256]{2,1,0:T(8,128)(2,1)} %shares.2), calls=%async_computation.1 | async-start | bytes 524288 | tf_op jit(solution)/shard_map/all_to_all | solution.py:413
  112.4 0.0 copy-done.6
  112.5 0.0 copy-done.9
  112.5 4.6 %scatter.11.local_ref = f32[2048,256]{1,0:T(8,128)} custom-call(s32[4,3072]{1,0:T(4,128)S(1)} %copy-done.9, bf16[256,3072]{1,0:T(8,128)(2,1)S(1)} %copy-done.6), custom_call_target="tpu_custom_call" | custom-call | flops 1099511627776 | bytes 4294967296 | tf_op jit(solution)/shard_map/scatter/pallas_call | solution.py:263
  117.1 3.8 %all-to-all-done.1.pieces_ref = bf16[4,128,256]{2,1,0:T(8,128)(2,1)} async-done(((bf16[4,128,256]{2,1,0:T(8,128)(2,1)}), bf16[4,128,256]{2,1,0:T(8,128)(2,1)}, u32[]{:S(2)}, u32[]{:S(2)}) %all-to-all-start.1) | async-done | bytes 262176 | tf_op jit(solution)/shard_map/all_to_all | solution.py:413
  120.9 0.0 copy-start.1
  120.9 0.0 copy-start.5
  120.9 1.9 %shares.3 = bf16[8,128,256]{2,1,0:T(8,128)(2,1)} custom-call(bf16[4,128,256]{2,1,0:T(8,128)(2,1)} %all-to-all-done.1.pieces_ref), custom_call_target="tpu_custom_call" | custom-call | flops 1099511627776 | bytes 4294967296 | tf_op jit(solution)/shard_map/shares/pallas_call | solution.py:340
  122.8 4.2 %all-to-all-start.2 = ((bf16[8,128,256]{2,1,0:T(8,128)(2,1)}), bf16[8,128,256]{2,1,0:T(8,128)(2,1)}, u32[]{:S(2)}, u32[]{:S(2)}) async-start(bf16[8,128,256]{2,1,0:T(8,128)(2,1)} %shares.3), calls=%async_computation.2 | async-start | bytes 1048576 | tf_op jit(solution)/shard_map/all_to_all | solution.py:413
  126.9 0.0 collective-permute-done.5.outer_ref
  127.0 0.0 collective-permute-done.6.back_ref
  127.0 0.0 copy-done.1
  127.0 0.0 copy-done.5
  127.0 0.0 copy-start.4
  127.0 4.1 %update.1 = (bf16[2048,256]{1,0:T(8,128)(2,1)}, f32[1,2048]{1,0:T(1,128)}) custom-call(s32[1]{0:T(128)} %bitcast.home_ref, bf16[2048,256]{1,0:T(8,128)(2,1)S(1)} %copy-done.1, f32[1,2048]{1,0:T(1,128)S(1)} %bitcast.8, f32[2048,256]{1,0:T(8,128)} %scatter.11.local_ref, bf16[2048,256]{1,0:T(8,128)(2,1)} %collective-permute-done.5.outer_ref, ...), custom_call_target="tpu_custom_call" | custom-call | flops 1099511627776 | bytes 4294967296 | tf_op jit(solution)/shard_map/update/pallas_call | solution.py:297
  131.1 5.1 %all-to-all-done.2 = bf16[8,128,256]{2,1,0:T(8,128)(2,1)} async-done(((bf16[8,128,256]{2,1,0:T(8,128)(2,1)}), bf16[8,128,256]{2,1,0:T(8,128)(2,1)}, u32[]{:S(2)}, u32[]{:S(2)}) %all-to-all-start.2) | async-done | bytes 524320 | tf_op jit(solution)/shard_map/all_to_all | solution.py:413
  136.2 0.0 copy-done.4
  136.2 2.5 %relation.1 = (f32[1000,256]{1,0:T(8,128)}, f32[1,1000]{1,0:T(1,128)}) custom-call(f32[1000,256]{1,0:T(8,128)S(1)} %copy-done.4, f32[1,1024]{1,0:T(1,128)S(1)} %pad.4.acc_ref, bf16[1024,256]{1,0:T(8,128)(2,1)} %bitcast.6.total_ref), custom_call_target="tpu_custom_call" | custom-call | flops 1099511627776 | bytes 4294967296 | tf_op jit(solution)/shard_map/relation/pallas_call | solution.py:321
  (1 shorter events, 0.0 us)
Async XLA Ops:
  0.6 15.8 %collective-permute-start.1 = (bf16[2048,256]{1,0:T(8,128)(2,1)}, bf16[2048,256]{1,0:T(8,128)(2,1)}, u32[]{:S(2)}, u32[]{:S(2)}) collective-permute-start(bf16[2048,256]{1,0:T(8,128)(2,1)} %entity_ref.1), channel_id=1, source_target_pairs={{0,8},{1,9},{2,10},{3,11},{4,12},{5,13},{6,14},{7,15},{8,16},{9,17... | collective-permute-start | bytes 3145736 | tf_op jit(solution)/shard_map/ppermute | solution.py:373
  1.1 31.8 %collective-permute-start = (bf16[2048,256]{1,0:T(8,128)(2,1)}, bf16[2048,256]{1,0:T(8,128)(2,1)}, u32[]{:S(2)}, u32[]{:S(2)}) collective-permute-start(bf16[2048,256]{1,0:T(8,128)(2,1)} %entity_ref.1), channel_id=1, source_target_pairs={{0,8},{1,9},{2,10},{3,11},{4,0},{5,1},{6,2},{7,3},{8,12},{9,13},{1... | collective-permute-start | bytes 3145736 | tf_op jit(solution)/shard_map/ppermute | solution.py:373
  3.8 1.5 %copy-start.3 = (f32[1000,256]{1,0:T(8,128)S(1)}, f32[1000,256]{1,0:T(8,128)}, u32[]{:S(2)}) copy-start(f32[1000,256]{1,0:T(8,128)} %relation_ref.3) | copy-start | bytes 3072004
  5.3 0.8 copy-start.7
  6.1 10.3 %copy-start.8 = (s32[4,3072]{1,0:T(4,128)S(1)}, s32[4,3072]{1,0:T(4,128)}, u32[]{:S(2)}) copy-start(s32[4,3072]{1,0:T(4,128)} %get-tuple-element.37.ids_ref.refs_0_.refs_2_) | copy-start | bytes 147460
  32.9 9.8 %collective-permute-start.2 = (bf16[2048,256]{1,0:T(8,128)(2,1)}, bf16[2048,256]{1,0:T(8,128)(2,1)}, u32[]{:S(2)}, u32[]{:S(2)}) collective-permute-start(bf16[2048,256]{1,0:T(8,128)(2,1)} %collective-permute-done.met_ref), channel_id=1, source_target_pairs={{0,8},{1,9},{2,10},{3,11},{12,4},{13,5},{14,6},{15,7},{16,24},{17,... | collective-permute-start | bytes 3145736 | tf_op jit(solution)/shard_map/ppermute | solution.py:373
  38.1 4.6 %collective-permute-start.3 = (s32[4,3072]{1,0:T(4,128)}, s32[4,3072]{1,0:T(4,128)}, u32[]{:S(2)}, u32[]{:S(2)}) collective-permute-start(s32[4,3072]{1,0:T(4,128)} %get-tuple-element.42.ids_ref), channel_id=1, source_target_pairs={{4,8},{5,9},{6,10},{7,11},{8,4},{9,5},{10,6},{11,7},{20,24},{21,25... | collective-permute-start | bytes 147464 | tf_op jit(solution)/shard_map/ppermute | solution.py:373
  39.4 3.4 %copy-start = (bf16[2048,256]{1,0:T(8,128)(2,1)S(1)}, bf16[2048,256]{1,0:T(8,128)(2,1)}, u32[]{:S(2)}) copy-start(bf16[2048,256]{1,0:T(8,128)(2,1)} %entity_ref.1) | copy-start | bytes 3145732
  65.9 6.4 %copy-start.10 = (f32[1000]{0:T(1024)S(1)}, f32[1000]{0:T(1024)}, u32[]{:S(2)}) copy-start(f32[1000]{0:T(1024)} %param.11) | copy-start | bytes 12004
  71.0 1.3 copy-start.2
  71.0 4.6 %collective-permute-start.4 = (bf16[2048,256]{1,0:T(8,128)(2,1)S(1)}, bf16[2048,256]{1,0:T(8,128)(2,1)S(1)}, u32[]{:S(2)}, u32[]{:S(2)}) collective-permute-start(bf16[2048,256]{1,0:T(8,128)(2,1)S(1)} %scatter.7.inner_ref), channel_id=1, source_target_pairs={{4,12},{5,13},{6,14},{7,15},{8,0},{9,1},{10,2},{11,3},{20,28},{21,... | collective-permute-start | bytes 3145736 | tf_op jit(solution)/shard_map/ppermute | solution.py:373
  75.5 1.0 copy-start.11
  86.2 40.7 %collective-permute-start.6 = (bf16[2048,256]{1,0:T(8,128)(2,1)}, bf16[2048,256]{1,0:T(8,128)(2,1)}, u32[]{:S(2)}, u32[]{:S(2)}) collective-permute-start(bf16[2048,256]{1,0:T(8,128)(2,1)} %scatter.8), channel_id=1, source_target_pairs={{0,4},{1,5},{2,6},{3,7},{4,12},{5,13},{6,14},{7,15},{8,0},{9,1},{1... | collective-permute-start | bytes 3145736 | tf_op jit(solution)/shard_map/ppermute | solution.py:373
  91.1 15.4 %all-to-all-start = ((bf16[8,128,256]{2,1,0:T(8,128)(2,1)}), bf16[8,128,256]{2,1,0:T(8,128)(2,1)}, u32[]{:S(2)}, u32[]{:S(2)}) async-start(bf16[8,128,256]{2,1,0:T(8,128)(2,1)} %bitcast.3), calls=%async_computation | async-start | bytes 1048576 | tf_op jit(solution)/shard_map/all_to_all | solution.py:413
  105.0 21.9 %collective-permute-start.5 = (bf16[2048,256]{1,0:T(8,128)(2,1)}, bf16[2048,256]{1,0:T(8,128)(2,1)}, u32[]{:S(2)}, u32[]{:S(2)}) collective-permute-start(bf16[2048,256]{1,0:T(8,128)(2,1)} %scatter.10), channel_id=1, source_target_pairs={{0,24},{1,25},{2,26},{3,27},{4,28},{5,29},{6,30},{7,31},{8,0},{9,1... | collective-permute-start | bytes 3145736 | tf_op jit(solution)/shard_map/ppermute | solution.py:373
  106.5 6.0 %copy-start.6 = (bf16[256,3072]{1,0:T(8,128)(2,1)S(1)}, bf16[256,3072]{1,0:T(8,128)(2,1)}, u32[]{:S(2)}) copy-start(bf16[256,3072]{1,0:T(8,128)(2,1)} %get-tuple-element.61.refs_1_) | copy-start | bytes 4718596
  106.5 6.0 %copy-start.9 = (s32[4,3072]{1,0:T(4,128)S(1)}, s32[4,3072]{1,0:T(4,128)}, u32[]{:S(2)}) copy-start(s32[4,3072]{1,0:T(4,128)} %get-tuple-element.37.ids_ref.refs_0_.refs_2_) | copy-start | bytes 147460
  108.4 12.5 %all-to-all-start.1 = ((bf16[4,128,256]{2,1,0:T(8,128)(2,1)}), bf16[4,128,256]{2,1,0:T(8,128)(2,1)}, u32[]{:S(2)}, u32[]{:S(2)}) async-start(bf16[4,128,256]{2,1,0:T(8,128)(2,1)} %shares.2), calls=%async_computation.1 | async-start | bytes 524288 | tf_op jit(solution)/shard_map/all_to_all | solution.py:413
  120.9 6.1 %copy-start.1 = (bf16[2048,256]{1,0:T(8,128)(2,1)S(1)}, bf16[2048,256]{1,0:T(8,128)(2,1)}, u32[]{:S(2)}) copy-start(bf16[2048,256]{1,0:T(8,128)(2,1)} %entity_ref.1) | copy-start | bytes 3145732
  120.9 6.1 %copy-start.5 = (f32[2048]{0:T(1024)S(1)}, f32[2048]{0:T(1024)}, u32[]{:S(2)}) copy-start(f32[2048]{0:T(1024)} %param.9) | copy-start | bytes 24580
  122.8 13.4 %all-to-all-start.2 = ((bf16[8,128,256]{2,1,0:T(8,128)(2,1)}), bf16[8,128,256]{2,1,0:T(8,128)(2,1)}, u32[]{:S(2)}, u32[]{:S(2)}) async-start(bf16[8,128,256]{2,1,0:T(8,128)(2,1)} %shares.3), calls=%async_computation.2 | async-start | bytes 1048576 | tf_op jit(solution)/shard_map/all_to_all | solution.py:413
  127.0 9.2 %copy-start.4 = (f32[1000,256]{1,0:T(8,128)S(1)}, f32[1000,256]{1,0:T(8,128)}, u32[]{:S(2)}) copy-start(f32[1000,256]{1,0:T(8,128)} %relation_ref.3) | copy-start | bytes 3072004

commit v5 on v4

--- a/solution.py
+++ b/solution.py
@@ -402,9 +402,12 @@
 
     left_one = scatter_call([(ids_one, 0, dl_one)], rows, [bf16])
     guest_left = send(left_one, neighbour, guest)
+    left_one, dp_one = lax.optimization_barrier((left_one, dp_one))
+    rel_sum = scatter_call([(ids_one, 1, dp_one)], rel_rows, [bf16], [rel_part])
+    rel_sum, dt_one = lax.optimization_barrier((rel_sum, dt_one))
     d_right_one = scatter_call([(ids_one, 2, dt_one), (ids_one, 3, dc_one)], rows, [bf16], [guest_left])
     back = send(d_right_one, parting)
-    d_right_one, dp_one, dt_two, dl_two = lax.optimization_barrier((d_right_one, dp_one, dt_two, dl_two))
+    d_right_one, rel_sum, dt_two, dl_two = lax.optimization_barrier((d_right_one, rel_sum, dt_two, dl_two))
 
     planes = [[g * doms + q + x for g in range(groups) for x in range(2)] for q in range(0, doms, 2)]
     stacks = [[g * doms + q + x for q in range(0, doms, 2)] for g in range(groups) for x in range(2)]
@@ -412,9 +415,7 @@
     def exchange(pieces, sets):
         return lax.all_to_all(pieces, axes, 0, 0, axis_index_groups=sets, tiled=True)
 
-    rel_sum = scatter_call([(ids_one, 1, dp_one)], rel_rows, [bf16], [rel_part])
     shares = exchange(rel_sum.reshape(2 * groups, -1, features), planes)
-    rel_sum, dt_two = lax.optimization_barrier((rel_sum, dt_two))
     d_right_two = scatter_call([(ids_two, 2, dt_two), (ids_two, 3, dc_two)], rows, [bf16])
     back_outer = send(d_right_two, lambda g, d: (g - 1, d))
     shares, d_right_two = lax.optimization_barrier((shares, d_right_two))

time: 139 us -> 140 us (level)
  waiting for transfers between devices: 12.2 us -> 10.2 us
  starting transfers between devices: 25.7 us -> 27.6 us
    ppermute x7, waiting for transfers between devices: 3.24 us -> 0.02 us  [send(): return lax.ppermute(block, axes, route)]
    ppermute x7, starting transfers between devices: 13.1 us -> 15.1 us  [send(): return lax.ppermute(block, axes, route)]
  transfers between devices with their start and end apart: 10 -> 10, of which waited for: 3 -> 2; matrix products, arithmetic and copies ran while one was open for 0% -> 0% of each run, Pallas kernels for 42% -> 42%
where the time goes in v5:
time: 140 us; the launch traced here: 139 us
  Pallas kernels  99.3 us (71%)
  starting transfers between devices  27.6 us (20%)
  waiting for transfers between devices  10.2 us (7%)
    pallas_call x6, Pallas kernels, scatter_call(): pl.pallas_call(kernel, grid=(rows // chunk,), in_specs=specs, out_specs=[...  37.3 us
    pallas_call x1, Pallas kernels, paired_call(): pl.pallas_call(functools.partial(paired_kernel, span), grid=(edges // wid...  23.2 us
    pallas_call x1, Pallas kernels, gradient_call(): pl.pallas_call(functools.partial(gradient_kernel, span), grid=(edges // w...  16.6 us
    ppermute x7, starting transfers between devices, send(): return lax.ppermute(block, axes, route)  15.1 us
    all_to_all x3, starting transfers between devices, exchange(): lax.all_to_all(pieces, axes, 0, 0, axis_index_groups=sets, tiled=True)  12.5 us
    pallas_call x1, Pallas kernels, query_call(): pl.pallas_call(query_kernel, grid=(edges // width,), in_specs=[across(4,...  10.3 us
    all_to_all x3, waiting for transfers between devices, exchange(): lax.all_to_all(pieces, axes, 0, 0, axis_index_groups=sets, tiled=True)  10.2 us
    pallas_call x1, Pallas kernels, update_call(): pl.pallas_call(update_kernel, grid=(rows // chunk,), in_specs=[pl.BlockSp...  4.07 us
  transfers between devices with their start and end apart: 10, of which 2 were waited for; matrix products, arithmetic and copies ran while one was open for 0% of the time, Pallas kernels for 42%

profile of v5, /device:TPU:0, one launch (start us, length us, event | category | flops | bytes accessed | tf_op | source)
XLA Modules:
  0.0 138.8 jit_solution(10382097810703773627)
XLA Ops:
  0.6 0.5 collective-permute-start.1
  1.1 2.6 %collective-permute-start = (bf16[2048,256]{1,0:T(8,128)(2,1)}, bf16[2048,256]{1,0:T(8,128)(2,1)}, u32[]{:S(2)}, u32[]{:S(2)}) collective-permute-start(bf16[2048,256]{1,0:T(8,128)(2,1)} %entity_ref.1), channel_id=1, source_target_pairs={{0,8},{1,9},{2,10},{3,11},{4,0},{5,1},{6,2},{7,3},{8,12},{9,13},{1... | collective-permute-start | bytes 3145736 | tf_op jit(solution)/shard_map/ppermute | solution.py:373
  3.8 0.0 copy-start.2
  3.8 1.5 %lines.1 = (s32[4,3072]{1,0:T(4,128)}, s32[4,3072]{1,0:T(4,128)}) custom-call(s32[1,2,3072]{2,1,0:T(2,128)} %source_ref.1, s32[1,2,3072]{2,1,0:T(2,128)} %rel_ref.1, s32[1,2,3072]{2,1,0:T(2,128)} %target_ref.1, s32[1,6,2,512]{3,2,1,0:T(2,128)} %bitcast.10), custom_call_target="tpu_custom_call" | custom-call | flops 1099511627776 | bytes 4294967296 | tf_op jit(solution)/shard_map/lines/pallas_call | solution.py:105
  5.3 0.0 copy-done.2
  5.3 0.0 copy-start.6
  5.3 0.8 copy-done.6
  6.1 0.0 copy-start.9
  6.1 0.0 copy-start.7
  6.1 10.3 %queries.1 = (bf16[256,3072]{1,0:T(8,128)(2,1)}, f32[256,3072]{1,0:T(8,128)}, bf16[256,3072]{1,0:T(8,128)(2,1)}, bf16[512,1024]{1,0:T(8,128)(2,1)}) custom-call(s32[4,3072]{1,0:T(4,128)S(1)} %copy-done.6, bf16[2048,256]{1,0:T(8,128)(2,1)} %entity_ref.1, f32[1000,256]{1,0:T(8,128)S(1)} %copy-done.2), custom_call_target="tpu_custom_call" | custom-call | flops 1099511627776 | bytes 4294967296 | tf_op jit(solution)/shard_map/queries/pallas_call | solution.py:182
  16.4 0.0 copy-done.9
  16.4 0.0 collective-permute-done.1.partner_ref
  16.5 0.0 copy-done.7
  16.5 16.6 %gradients.1 = (bf16[256,3072]{1,0:T(8,128)(2,1)}, bf16[256,3072]{1,0:T(8,128)(2,1)}, bf16[256,3072]{1,0:T(8,128)(2,1)}, bf16[256,3072]{1,0:T(8,128)(2,1)}) custom-call(s32[4,3072]{1,0:T(4,128)S(1)} %copy-done.7, bf16[256,3072]{1,0:T(8,128)(2,1)} %get-tuple-element.41.heads_ref, f32[256,3072]{1,0:T(8,128)} %get-tuple-element.42.rel_ref, ...), custom_call_target="tpu_custom_call" | custom-call | flops 1099511627776 | bytes 4294967296 | tf_op jit(solution)/shard_map/gradients/pallas_call | solution.py:203
  33.1 0.0 collective-permute-done.met_ref
  33.1 5.2 %collective-permute-start.2 = (bf16[2048,256]{1,0:T(8,128)(2,1)}, bf16[2048,256]{1,0:T(8,128)(2,1)}, u32[]{:S(2)}, u32[]{:S(2)}) collective-permute-start(bf16[2048,256]{1,0:T(8,128)(2,1)} %collective-permute-done.met_ref), channel_id=1, source_target_pairs={{0,8},{1,9},{2,10},{3,11},{12,4},{13,5},{14,6},{15,7},{16,24},{17,... | collective-permute-start | bytes 3145736 | tf_op jit(solution)/shard_map/ppermute | solution.py:373
  38.3 1.3 collective-permute-start.3
  39.6 0.0 copy-start
  39.6 3.3 %scatter.6.refs_2_ = f32[1024,256]{1,0:T(8,128)S(1)} custom-call(s32[4,3072]{1,0:T(4,128)S(1)} %copy-done.7, bf16[256,3072]{1,0:T(8,128)(2,1)} %get-tuple-element.47.refs_1_), custom_call_target="tpu_custom_call" | custom-call | flops 1099511627776 | bytes 4294967296 | tf_op jit(solution)/shard_map/scatter/pallas_call | solution.py:263
  42.9 0.0 collective-permute-done.3.sent_ref
  42.9 0.0 collective-permute-done.2.passed_ref
  42.9 0.0 copy-done
  42.9 23.2 %paired.1 = (bf16[256,3072]{1,0:T(8,128)(2,1)}, bf16[256,3072]{1,0:T(8,128)(2,1)}, bf16[256,3072]{1,0:T(8,128)(2,1)}, bf16[256,3072]{1,0:T(8,128)(2,1)}, s32[4,3072]{1,0:T(4,128)S(1)}) custom-call(s32[1]{0:T(128)} %bitcast.home_ref, s32[4,3072]{1,0:T(4,128)} %get-tuple-element.45.ids_ref, s32[4,3072]{1,0:T(4,128)} %collective-permute-done.3.sent_ref, ...), custom_call_target="tpu_custom_call" | custom-call | flops 1099511627776 | bytes 4294967296 | tf_op jit(solution)/shard_map/paired/pallas_call | solution.py:219
  66.1 5.9 %scatter.7.inner_ref = bf16[2048,256]{1,0:T(8,128)(2,1)} custom-call(s32[4,3072]{1,0:T(4,128)S(1)} %get-tuple-element.51.refs_0_.refs_2_, bf16[256,3072]{1,0:T(8,128)(2,1)} %get-tuple-element.52.refs_1_), custom_call_target="tpu_custom_call" | custom-call | flops 1099511627776 | bytes 4294967296 | tf_op jit(solution)/shard_map/scatter/pallas_call | solution.py:263
  72.0 1.3 collective-permute-start.4
  73.3 4.0 %scatter.8 = bf16[1024,256]{1,0:T(8,128)(2,1)} custom-call(s32[4,3072]{1,0:T(4,128)S(1)} %get-tuple-element.51.refs_0_.refs_2_, bf16[256,3072]{1,0:T(8,128)(2,1)} %get-tuple-element.54.refs_1_, f32[1024,256]{1,0:T(8,128)S(1)} %scatter.6.refs_2_), custom_call_target="tpu_custom_call" | custom-call | flops 1099511627776 | bytes 4294967296 | tf_op jit(solution)/shard_map/scatter/pallas_call | solution.py:263
  77.3 0.0 collective-permute-done.4.refs_4_
  77.3 9.8 %scatter.9 = bf16[2048,256]{1,0:T(8,128)(2,1)} custom-call(s32[4,3072]{1,0:T(4,128)S(1)} %get-tuple-element.51.refs_0_.refs_2_, bf16[256,3072]{1,0:T(8,128)(2,1)} %get-tuple-element.57.refs_1_, s32[4,3072]{1,0:T(4,128)S(1)} %get-tuple-element.51.refs_0_.refs_2_, bf16[256,3072]{1,0:T(8,128)(2,1)} %get-tuple-element.58.refs_3_, ...), custom_call_target="tpu_custom_call" | custom-call | flops 1099511627776 | bytes 4294967296 | tf_op jit(solution)/shard_map/scatter/pallas_call | solution.py:263
  87.1 2.8 %collective-permute-start.6 = (bf16[2048,256]{1,0:T(8,128)(2,1)}, bf16[2048,256]{1,0:T(8,128)(2,1)}, u32[]{:S(2)}, u32[]{:S(2)}) collective-permute-start(bf16[2048,256]{1,0:T(8,128)(2,1)} %scatter.9), channel_id=1, source_target_pairs={{0,4},{1,5},{2,6},{3,7},{4,12},{5,13},{6,14},{7,15},{8,0},{9,1},{1... | collective-permute-start | bytes 3145736 | tf_op jit(solution)/shard_map/ppermute | solution.py:373
  89.9 4.4 %all-to-all-start = ((bf16[8,128,256]{2,1,0:T(8,128)(2,1)}), bf16[8,128,256]{2,1,0:T(8,128)(2,1)}, u32[]{:S(2)}, u32[]{:S(2)}) async-start(bf16[8,128,256]{2,1,0:T(8,128)(2,1)} %bitcast.3), calls=%async_computation | async-start | bytes 1048576 | tf_op jit(solution)/shard_map/all_to_all | solution.py:416
  94.3 9.6 %scatter.10 = bf16[2048,256]{1,0:T(8,128)(2,1)} custom-call(s32[4,3072]{1,0:T(4,128)S(1)} %copy-done.7, bf16[256,3072]{1,0:T(8,128)(2,1)} %get-tuple-element.63.refs_1_, s32[4,3072]{1,0:T(4,128)S(1)} %copy-done.7, bf16[256,3072]{1,0:T(8,128)(2,1)} %get-tuple-element.64.refs_3_), custom_call_target="tpu_custom_call" | custom-call | flops 1099511627776 | bytes 4294967296 | tf_op jit(solution)/shard_map/scatter/pallas_call | solution.py:263
  103.9 1.4 %collective-permute-start.5 = (bf16[2048,256]{1,0:T(8,128)(2,1)}, bf16[2048,256]{1,0:T(8,128)(2,1)}, u32[]{:S(2)}, u32[]{:S(2)}) collective-permute-start(bf16[2048,256]{1,0:T(8,128)(2,1)} %scatter.10), channel_id=1, source_target_pairs={{0,24},{1,25},{2,26},{3,27},{4,28},{5,29},{6,30},{7,31},{8,0},{9,1... | collective-permute-start | bytes 3145736 | tf_op jit(solution)/shard_map/ppermute | solution.py:373
  105.3 0.0 all-to-all-done.pieces_ref
  105.3 0.0 copy-start.5
  105.3 0.0 copy-start.8
  105.3 1.9 %shares.2 = bf16[4,128,256]{2,1,0:T(8,128)(2,1)} custom-call(bf16[8,128,256]{2,1,0:T(8,128)(2,1)} %all-to-all-done.pieces_ref), custom_call_target="tpu_custom_call" | custom-call | flops 1099511627776 | bytes 4294967296 | tf_op jit(solution)/shard_map/shares/pallas_call | solution.py:340
  107.2 4.0 %all-to-all-start.1 = ((bf16[4,128,256]{2,1,0:T(8,128)(2,1)}), bf16[4,128,256]{2,1,0:T(8,128)(2,1)}, u32[]{:S(2)}, u32[]{:S(2)}) async-start(bf16[4,128,256]{2,1,0:T(8,128)(2,1)} %shares.2), calls=%async_computation.1 | async-start | bytes 524288 | tf_op jit(solution)/shard_map/all_to_all | solution.py:416
  111.3 0.0 copy-done.5
  111.3 0.0 copy-done.8
  111.3 4.6 %scatter.11.local_ref = f32[2048,256]{1,0:T(8,128)} custom-call(s32[4,3072]{1,0:T(4,128)S(1)} %copy-done.8, bf16[256,3072]{1,0:T(8,128)(2,1)S(1)} %copy-done.5), custom_call_target="tpu_custom_call" | custom-call | flops 1099511627776 | bytes 4294967296 | tf_op jit(solution)/shard_map/scatter/pallas_call | solution.py:263
  115.9 5.1 %all-to-all-done.1.pieces_ref = bf16[4,128,256]{2,1,0:T(8,128)(2,1)} async-done(((bf16[4,128,256]{2,1,0:T(8,128)(2,1)}), bf16[4,128,256]{2,1,0:T(8,128)(2,1)}, u32[]{:S(2)}, u32[]{:S(2)}) %all-to-all-start.1) | async-done | bytes 262176 | tf_op jit(solution)/shard_map/all_to_all | solution.py:416
  121.0 0.0 copy-start.1
  121.0 0.0 copy-start.4
  121.0 1.9 %shares.3 = bf16[8,128,256]{2,1,0:T(8,128)(2,1)} custom-call(bf16[4,128,256]{2,1,0:T(8,128)(2,1)} %all-to-all-done.1.pieces_ref), custom_call_target="tpu_custom_call" | custom-call | flops 1099511627776 | bytes 4294967296 | tf_op jit(solution)/shard_map/shares/pallas_call | solution.py:340
  122.8 4.1 %all-to-all-start.2 = ((bf16[8,128,256]{2,1,0:T(8,128)(2,1)}), bf16[8,128,256]{2,1,0:T(8,128)(2,1)}, u32[]{:S(2)}, u32[]{:S(2)}) async-start(bf16[8,128,256]{2,1,0:T(8,128)(2,1)} %shares.3), calls=%async_computation.2 | async-start | bytes 1048576 | tf_op jit(solution)/shard_map/all_to_all | solution.py:416
  127.0 0.0 collective-permute-done.5.outer_ref
  127.0 0.0 collective-permute-done.6.back_ref
  127.0 0.0 copy-done.1
  127.0 0.0 copy-done.4
  127.0 0.0 copy-start.3
  127.0 4.1 %update.1 = (bf16[2048,256]{1,0:T(8,128)(2,1)}, f32[1,2048]{1,0:T(1,128)}) custom-call(s32[1]{0:T(128)} %bitcast.home_ref, bf16[2048,256]{1,0:T(8,128)(2,1)S(1)} %copy-done.1, f32[1,2048]{1,0:T(1,128)S(1)} %bitcast.8, f32[2048,256]{1,0:T(8,128)} %scatter.11.local_ref, bf16[2048,256]{1,0:T(8,128)(2,1)} %collective-permute-done.5.outer_ref, ...), custom_call_target="tpu_custom_call" | custom-call | flops 1099511627776 | bytes 4294967296 | tf_op jit(solution)/shard_map/update/pallas_call | solution.py:297
  131.1 5.1 %all-to-all-done.2 = bf16[8,128,256]{2,1,0:T(8,128)(2,1)} async-done(((bf16[8,128,256]{2,1,0:T(8,128)(2,1)}), bf16[8,128,256]{2,1,0:T(8,128)(2,1)}, u32[]{:S(2)}, u32[]{:S(2)}) %all-to-all-start.2) | async-done | bytes 524320 | tf_op jit(solution)/shard_map/all_to_all | solution.py:416
  136.3 0.0 copy-done.3
  136.3 2.5 %relation.1 = (f32[1000,256]{1,0:T(8,128)}, f32[1,1000]{1,0:T(1,128)}) custom-call(f32[1000,256]{1,0:T(8,128)S(1)} %copy-done.3, f32[1,1024]{1,0:T(1,128)S(1)} %pad.4.acc_ref, bf16[1024,256]{1,0:T(8,128)(2,1)} %bitcast.6.total_ref), custom_call_target="tpu_custom_call" | custom-call | flops 1099511627776 | bytes 4294967296 | tf_op jit(solution)/shard_map/relation/pallas_call | solution.py:321
  (1 shorter events, 0.0 us)
Async XLA Ops:
  0.6 15.8 %collective-permute-start.1 = (bf16[2048,256]{1,0:T(8,128)(2,1)}, bf16[2048,256]{1,0:T(8,128)(2,1)}, u32[]{:S(2)}, u32[]{:S(2)}) collective-permute-start(bf16[2048,256]{1,0:T(8,128)(2,1)} %entity_ref.1), channel_id=1, source_target_pairs={{0,8},{1,9},{2,10},{3,11},{4,12},{5,13},{6,14},{7,15},{8,16},{9,17... | collective-permute-start | bytes 3145736 | tf_op jit(solution)/shard_map/ppermute | solution.py:373
  1.1 32.0 %collective-permute-start = (bf16[2048,256]{1,0:T(8,128)(2,1)}, bf16[2048,256]{1,0:T(8,128)(2,1)}, u32[]{:S(2)}, u32[]{:S(2)}) collective-permute-start(bf16[2048,256]{1,0:T(8,128)(2,1)} %entity_ref.1), channel_id=1, source_target_pairs={{0,8},{1,9},{2,10},{3,11},{4,0},{5,1},{6,2},{7,3},{8,12},{9,13},{1... | collective-permute-start | bytes 3145736 | tf_op jit(solution)/shard_map/ppermute | solution.py:373
  3.8 1.5 %copy-start.2 = (f32[1000,256]{1,0:T(8,128)S(1)}, f32[1000,256]{1,0:T(8,128)}, u32[]{:S(2)}) copy-start(f32[1000,256]{1,0:T(8,128)} %relation_ref.3) | copy-start | bytes 3072004
  5.3 0.8 copy-start.6
  6.1 10.3 %copy-start.9 = (f32[1000]{0:T(1024)S(1)}, f32[1000]{0:T(1024)}, u32[]{:S(2)}) copy-start(f32[1000]{0:T(1024)} %param.11) | copy-start | bytes 12004
  6.1 10.4 %copy-start.7 = (s32[4,3072]{1,0:T(4,128)S(1)}, s32[4,3072]{1,0:T(4,128)}, u32[]{:S(2)}) copy-start(s32[4,3072]{1,0:T(4,128)} %get-tuple-element.40.ids_ref.refs_0_.refs_2_) | copy-start | bytes 147460
  33.1 9.8 %collective-permute-start.2 = (bf16[2048,256]{1,0:T(8,128)(2,1)}, bf16[2048,256]{1,0:T(8,128)(2,1)}, u32[]{:S(2)}, u32[]{:S(2)}) collective-permute-start(bf16[2048,256]{1,0:T(8,128)(2,1)} %collective-permute-done.met_ref), channel_id=1, source_target_pairs={{0,8},{1,9},{2,10},{3,11},{12,4},{13,5},{14,6},{15,7},{16,24},{17,... | collective-permute-start | bytes 3145736 | tf_op jit(solution)/shard_map/ppermute | solution.py:373
  38.3 4.6 %collective-permute-start.3 = (s32[4,3072]{1,0:T(4,128)}, s32[4,3072]{1,0:T(4,128)}, u32[]{:S(2)}, u32[]{:S(2)}) collective-permute-start(s32[4,3072]{1,0:T(4,128)} %get-tuple-element.45.ids_ref), channel_id=1, source_target_pairs={{4,8},{5,9},{6,10},{7,11},{8,4},{9,5},{10,6},{11,7},{20,24},{21,25... | collective-permute-start | bytes 147464 | tf_op jit(solution)/shard_map/ppermute | solution.py:373
  39.6 3.4 %copy-start = (bf16[2048,256]{1,0:T(8,128)(2,1)S(1)}, bf16[2048,256]{1,0:T(8,128)(2,1)}, u32[]{:S(2)}) copy-start(bf16[2048,256]{1,0:T(8,128)(2,1)} %entity_ref.1) | copy-start | bytes 3145732
  72.0 5.3 %collective-permute-start.4 = (bf16[2048,256]{1,0:T(8,128)(2,1)}, bf16[2048,256]{1,0:T(8,128)(2,1)}, u32[]{:S(2)}, u32[]{:S(2)}) collective-permute-start(bf16[2048,256]{1,0:T(8,128)(2,1)} %scatter.7.inner_ref), channel_id=1, source_target_pairs={{4,12},{5,13},{6,14},{7,15},{8,0},{9,1},{10,2},{11,3},{20,28},{21,... | collective-permute-start | bytes 3145736 | tf_op jit(solution)/shard_map/ppermute | solution.py:373
  87.1 39.9 %collective-permute-start.6 = (bf16[2048,256]{1,0:T(8,128)(2,1)}, bf16[2048,256]{1,0:T(8,128)(2,1)}, u32[]{:S(2)}, u32[]{:S(2)}) collective-permute-start(bf16[2048,256]{1,0:T(8,128)(2,1)} %scatter.9), channel_id=1, source_target_pairs={{0,4},{1,5},{2,6},{3,7},{4,12},{5,13},{6,14},{7,15},{8,0},{9,1},{1... | collective-permute-start | bytes 3145736 | tf_op jit(solution)/shard_map/ppermute | solution.py:373
  89.9 15.4 %all-to-all-start = ((bf16[8,128,256]{2,1,0:T(8,128)(2,1)}), bf16[8,128,256]{2,1,0:T(8,128)(2,1)}, u32[]{:S(2)}, u32[]{:S(2)}) async-start(bf16[8,128,256]{2,1,0:T(8,128)(2,1)} %bitcast.3), calls=%async_computation | async-start | bytes 1048576 | tf_op jit(solution)/shard_map/all_to_all | solution.py:416
  103.9 23.1 %collective-permute-start.5 = (bf16[2048,256]{1,0:T(8,128)(2,1)}, bf16[2048,256]{1,0:T(8,128)(2,1)}, u32[]{:S(2)}, u32[]{:S(2)}) collective-permute-start(bf16[2048,256]{1,0:T(8,128)(2,1)} %scatter.10), channel_id=1, source_target_pairs={{0,24},{1,25},{2,26},{3,27},{4,28},{5,29},{6,30},{7,31},{8,0},{9,1... | collective-permute-start | bytes 3145736 | tf_op jit(solution)/shard_map/ppermute | solution.py:373
  105.3 6.0 %copy-start.5 = (bf16[256,3072]{1,0:T(8,128)(2,1)S(1)}, bf16[256,3072]{1,0:T(8,128)(2,1)}, u32[]{:S(2)}) copy-start(bf16[256,3072]{1,0:T(8,128)(2,1)} %get-tuple-element.66.refs_1_) | copy-start | bytes 4718596
  105.3 6.0 %copy-start.8 = (s32[4,3072]{1,0:T(4,128)S(1)}, s32[4,3072]{1,0:T(4,128)}, u32[]{:S(2)}) copy-start(s32[4,3072]{1,0:T(4,128)} %get-tuple-element.40.ids_ref.refs_0_.refs_2_) | copy-start | bytes 147460
  107.2 13.8 %all-to-all-start.1 = ((bf16[4,128,256]{2,1,0:T(8,128)(2,1)}), bf16[4,128,256]{2,1,0:T(8,128)(2,1)}, u32[]{:S(2)}, u32[]{:S(2)}) async-start(bf16[4,128,256]{2,1,0:T(8,128)(2,1)} %shares.2), calls=%async_computation.1 | async-start | bytes 524288 | tf_op jit(solution)/shard_map/all_to_all | solution.py:416
  121.0 6.0 %copy-start.1 = (bf16[2048,256]{1,0:T(8,128)(2,1)S(1)}, bf16[2048,256]{1,0:T(8,128)(2,1)}, u32[]{:S(2)}) copy-start(bf16[2048,256]{1,0:T(8,128)(2,1)} %entity_ref.1) | copy-start | bytes 3145732
  121.0 6.1 %copy-start.4 = (f32[2048]{0:T(1024)S(1)}, f32[2048]{0:T(1024)}, u32[]{:S(2)}) copy-start(f32[2048]{0:T(1024)} %param.9) | copy-start | bytes 24580
  122.8 13.4 %all-to-all-start.2 = ((bf16[8,128,256]{2,1,0:T(8,128)(2,1)}), bf16[8,128,256]{2,1,0:T(8,128)(2,1)}, u32[]{:S(2)}, u32[]{:S(2)}) async-start(bf16[8,128,256]{2,1,0:T(8,128)(2,1)} %shares.3), calls=%async_computation.2 | async-start | bytes 1048576 | tf_op jit(solution)/shard_map/all_to_all | solution.py:416
  127.0 9.2 %copy-start.3 = (f32[1000,256]{1,0:T(8,128)S(1)}, f32[1000,256]{1,0:T(8,128)}, u32[]{:S(2)}) copy-start(f32[1000,256]{1,0:T(8,128)} %relation_ref.3) | copy-start | bytes 3072004
